TPU v7x, 512 devices: a whole 4x8x8 slice. The times are simulated.
512 devices in a mesh: section: 8 (over z_hi, x), ctx: 64 (over y, z_lo, core).
Axes of the slice: x: 4, y: 8, z: 8 (z_hi: 2, z_lo: 4; z = z_hi * 4 + z_lo), core: 2. Of those that a mesh axis runs over, the one named last changes fastest.
Arguments:
- resid: bfloat16 [8, 16384, 4096], P('section', 'ctx'), may hold values from -16 to 16
- queries: bfloat16 [8, 16384, 512], P('section', 'ctx'), may hold values from -8 to 8
- keyvals: bfloat16 [8, 16384, 256], P('section', 'ctx'), may hold values from -8 to 8
- run_max: float32 [8, 16384, 4], P('section', 'ctx'), may hold values from 1 to 4
- run_sum: float32 [8, 16384, 4], P('section', 'ctx'), may hold values from 128 to 1024
- run_out: float32 [8, 16384, 512], P('section', 'ctx'), may hold values from -384 to 384
- span_pair: int32 [64, 2], replicated, may hold values from 0 to 127, as said below
- norm_gain: float32 [8, 4096], P('section'), may hold values from 0.5 to 1.5
- w_query: bfloat16 [8, 4096, 512], P('section', 'ctx'), may hold values from -0.095458984 to 0.095458984
- w_keyval: bfloat16 [8, 4096, 256], P('section', 'ctx'), may hold values from -0.095458984 to 0.095458984
- w_out: bfloat16 [8, 512, 4096], P('section', None, 'ctx'), may hold values from -0.59765625 to 0.59765625
Outputs:
- queries_next: bfloat16 [8, 16384, 512], P('section', 'ctx')
- keyvals_next: bfloat16 [8, 16384, 256], P('section', 'ctx')
- max_next: float32 [8, 16384, 4], P('section', 'ctx')
- sum_next: float32 [8, 16384, 4], P('section', 'ctx')
- out_next: float32 [8, 16384, 512], P('section', 'ctx')
Inputs may be any that keep to these rules, and one draw needn't show every extreme that they name: `span_pair`: each ctx index holds blocks c and 127 - c, its first column running once over 0 to 63.
All inputs are finite; a program needn't handle non-finite values.
Results may differ from a plain program's by a relative error of at most 0.005.
The roundings to bfloat16 on the way count: a program that leaves them out, or rounds other values in their place, can miss the bound.
Values may be sent and summed in bfloat16 or wider, within the bound.
No kernel may reach another device: no remote copies, remote signals or barrier semaphores. Data moves between devices by JAX's collectives and lax.ppermute only.
A program may use at most 64 MiB of HBM per device.

v0:
```python
import jax
import jax.numpy as jnp
from jax import lax
from jax.experimental import pallas as pl
from jax.experimental.pallas import tpu as pltpu
from jax.sharding import Mesh
from jax.sharding import PartitionSpec as P


HEAD = 128
QHEADS = 4
SECT = ("zh", "x")
CTX = ("y", "zl", "c")
NY, NZ, NC, NS = 8, 4, 2, 8
SHARD = 64
NX = 4
STARTS = (0, 128, 192)
BLOCK = NZ * NC * SHARD
NQ = QHEADS * HEAD
NKV = 2 * HEAD


def ring(count, steps):
    return [(source, (source + steps) % count) for source in range(count)]


def positions(span_ref, device, rows, axis):
    half = rows // 2
    shape = (rows, 1) if axis == 0 else (1, rows)
    offset = lax.broadcasted_iota(jnp.int32, shape, axis)
    first = span_ref[0, device] * half
    second = span_ref[1, device] * half - half
    return offset + jnp.where(offset < half, first, second)


def block_update(query, key, value, keep, old):
    scores = lax.dot_general(
        key, query, (((1,), (1,)), ((), ())), preferred_element_type=jnp.float32
    ) * HEAD ** (-0.5)
    masked = jnp.where(keep, scores, -1e30)
    old_max, old_sum, old_out = old
    new_max = jnp.maximum(old_max, jnp.max(masked, axis=0, keepdims=True))
    exp_scores = jnp.exp(masked - new_max)
    decay = jnp.exp(old_max - new_max)
    new_sum = old_sum * decay + jnp.sum(exp_scores, axis=0, keepdims=True)
    contrib = jnp.dot(value, exp_scores.astype(jnp.bfloat16), preferred_element_type=jnp.float32)
    new_out = contrib if old_out is None else old_out * decay + contrib
    return new_max, new_sum, new_out


def attend_kernel(index_ref, span_ref, query_ref, far_ref, near_ref, max_ref, sum_ref, out_ref, att_ref):
    count = NY * NZ * NC
    rows = query_ref.shape[0]
    mine = index_ref[0]
    pos_query = positions(span_ref, mine, rows, 1)
    blocks = []
    for hop, block_ref in ((2, far_ref), (1, near_ref)):
        keep = positions(span_ref, lax.rem(mine + hop, count), rows, 0) <= pos_query
        blocks.append((block_ref[:, :HEAD], block_ref[:, HEAD:].T, keep))
    for h in range(QHEADS):
        cols = slice(h * HEAD, (h + 1) * HEAD)
        state = max_ref[h : h + 1, :], sum_ref[h : h + 1, :], out_ref[:, cols].T
        for block in blocks:
            state = block_update(query_ref[:, cols], *block, state)
        att_ref[:, cols] = (state[2] / state[1]).T.astype(jnp.bfloat16)


def attend(my_index, spans, *operands):
    return pl.pallas_call(
        attend_kernel,
        out_shape=jax.ShapeDtypeStruct(operands[0].shape, jnp.bfloat16),
        in_specs=[pl.BlockSpec(memory_space=pltpu.SMEM)] * 2
        + [pl.BlockSpec(memory_space=pltpu.VMEM)] * len(operands),
        out_specs=pl.BlockSpec(memory_space=pltpu.VMEM),
        name="attend",
    )(my_index, spans, *operands)


def in_order(w_ref, y, cols):
    parts = []
    for z in range(NZ):
        for c in range(NC):
            start = ((y * NC + c) * NZ + z) * SHARD
            parts.append(w_ref[start : start + SHARD, cols])
    return jnp.concatenate(parts, axis=0)


def layer_kernel(
    place_ref,
    span_ref,
    att_ref,
    gain_ref,
    direct_ref,
    near_a_ref,
    near_b_ref,
    far_a_ref,
    far_b_ref,
    weight_ref,
    query_ref,
    keyval_ref,
    max_ref,
    sum_ref,
    wide_ref,
    resid_ref,
    out_ref,
    row_sems,
    out_sems,
):
    rows = query_ref.shape[0]
    by_near = place_ref[1] > 0

    def out_copy(y):
        block = pl.ds(y * BLOCK, BLOCK)
        return pltpu.make_async_copy(weight_ref.at[block, :], out_ref.at[block, :], out_sems.at[y])

    def row_copy(source, part):
        block = resid_ref.at[pl.ds(STARTS[part], source.shape[0]), :]
        return pltpu.make_async_copy(source, block, row_sems.at[part])

    out_copy(0).start()
    row_copy(direct_ref, 0).start()

    @pl.when(by_near)
    def _():
        row_copy(near_a_ref, 1).start()
        row_copy(near_b_ref, 2).start()

    @pl.when(jnp.logical_not(by_near))
    def _():
        row_copy(far_a_ref, 1).start()
        row_copy(far_b_ref, 2).start()

    for y in range(1, NY):
        out_copy(y).start()
    for part, source in enumerate((direct_ref, near_a_ref, near_b_ref)):
        row_copy(source, part).wait()

    total = None
    for y in range(NY):
        cols = slice(y * BLOCK, (y + 1) * BLOCK)
        out_copy(y).wait()
        projected = lax.dot_general(
            att_ref[...],
            in_order(out_ref, y, slice(NQ + NKV, None)),
            (((1,), (1,)), ((), ())),
            preferred_element_type=jnp.float32,
        )
        finished = (resid_ref[:, cols].astype(jnp.float32) + projected).astype(jnp.bfloat16)
        square = finished.astype(jnp.float32)
        square = square * square
        part = sum(square[:, j * HEAD : (j + 1) * HEAD] for j in range(BLOCK // HEAD))
        total = part if total is None else total + part
        resid_ref[:, cols] = finished

    scale = lax.rsqrt(jnp.sum(total, axis=-1, keepdims=True) / (NY * BLOCK) + 1e-05)
    total = None
    for y in range(NY):
        cols = slice(y * BLOCK, (y + 1) * BLOCK)
        value = resid_ref[:, cols].astype(jnp.float32) * scale * gain_ref[:, cols]
        part = jnp.dot(
            value.astype(jnp.bfloat16), in_order(out_ref, y, slice(0, NQ + NKV)), preferred_element_type=jnp.float32
        )
        total = part if total is None else total + part

    query = total[:, :NQ].astype(jnp.bfloat16)
    keyval = total[:, NQ:].astype(jnp.bfloat16)
    query_ref[...] = query
    keyval_ref[...] = keyval
    mine = place_ref[0]
    keep = positions(span_ref, mine, rows, 0) <= positions(span_ref, mine, rows, 1)
    key = keyval[:, :HEAD]
    value = keyval[:, HEAD:].T
    for h in range(QHEADS):
        cols = slice(h * HEAD, (h + 1) * HEAD)
        state = jnp.full((1, rows), -1e30, jnp.float32), jnp.zeros((1, rows), jnp.float32), None
        state = block_update(query[:, cols], key, value, keep, state)
        max_ref[h : h + 1, :] = state[0]
        sum_ref[h : h + 1, :] = state[1]
        wide_ref[:, cols] = state[2].T


def layer(place, spans, attended, gain, parts, weights):
    rows = attended.shape[0]
    depth = weights.shape[0]
    smem = pl.BlockSpec(memory_space=pltpu.SMEM)
    vmem = pl.BlockSpec(memory_space=pltpu.VMEM)
    anywhere = pl.BlockSpec(memory_space=pl.ANY)
    stat = jax.ShapeDtypeStruct((QHEADS, rows), jnp.float32)
    return pl.pallas_call(
        layer_kernel,
        out_shape=(
            jax.ShapeDtypeStruct((rows, NQ), jnp.bfloat16),
            jax.ShapeDtypeStruct((rows, NKV), jnp.bfloat16),
            stat,
            stat,
            jax.ShapeDtypeStruct((rows, NQ), jnp.float32),
        ),
        in_specs=[smem, smem, vmem, vmem] + [anywhere] * (len(parts) + 1),
        out_specs=(vmem,) * 5,
        scratch_shapes=[
            pltpu.VMEM((rows, depth), jnp.bfloat16),
            pltpu.VMEM(weights.shape, jnp.bfloat16),
            pltpu.SemaphoreType.DMA((len(STARTS),)),
            pltpu.SemaphoreType.DMA((NY,)),
        ],
        name="layer",
    )(place, spans, attended, gain, *parts, weights)


def per_device(
    resid,
    queries,
    keyvals,
    run_max,
    run_sum,
    run_out,
    span_pair,
    norm_gain,
    w_query,
    w_keyval,
    w_out,
):
    count = NY * NZ * NC
    my_index = lax.axis_index(CTX).astype(jnp.int32)
    my_x = lax.axis_index("x").astype(jnp.int32)
    spans = span_pair.T

    out_shard = lax.ppermute(w_out[0].T, SECT, ring(NS, 1))
    next_shard = jnp.concatenate([w_query[0], w_keyval[0]], axis=1)

    def along_z(shard):
        copies = jnp.broadcast_to(shard, (NZ, *shard.shape))
        return lax.all_to_all(copies, "zl", 0, 0, tiled=True).reshape(NZ * SHARD, -1)

    next_rows = along_z(next_shard)
    out_rows = along_z(out_shard)
    shards = jnp.concatenate([next_rows, out_rows], axis=1)
    weights = lax.all_gather(shards, ("y", "c"), axis=0, tiled=True)

    turn = [(s, (s + 1) % NX + s // NX * NX) for s in range(NS)]
    near_a = lax.ppermute(resid[0, STARTS[1] : STARTS[2]], SECT, turn)
    direct = lax.ppermute(resid[0, : STARTS[1]], SECT, ring(NS, 1))
    near_b = lax.ppermute(resid[0, STARTS[2] :], SECT, turn)
    near_block = lax.ppermute(keyvals[0], CTX, ring(count, -1))
    far_block = lax.ppermute(keyvals[0], CTX, ring(count, -2))
    attended = attend(
        my_index.reshape(1), spans, queries[0], far_block, near_block,
        run_max[0].T, run_sum[0].T, run_out[0],
    )
    attended_sent = lax.ppermute(attended, SECT, ring(NS, 1))
    far_a = lax.ppermute(near_a, SECT, [(0, NX), (NX, 0)])
    leaving_b, far_a = lax.optimization_barrier((near_b, far_a))
    far_b = lax.ppermute(leaving_b, SECT, [(0, NX), (NX, 0)])
    place = jnp.stack([my_index, (my_x > 0).astype(jnp.int32)])
    query_new, keyval_new, max_new, sum_new, out_new = layer(
        place, spans, attended_sent, norm_gain, (direct, near_a, near_b, far_a, far_b), weights
    )
    return (query_new[None], keyval_new[None], max_new.T[None], sum_new.T[None], out_new[None])


def solution(mesh):
    fine = Mesh(mesh.devices.reshape(2, NX, NY, NZ, NC), (*SECT, *CTX))
    rows = P(SECT, CTX, None)
    return jax.shard_map(
        per_device,
        mesh=fine,
        in_specs=(*[rows] * 6, P(), P(SECT, None), rows, rows, P(SECT, None, CTX)),
        out_specs=(rows,) * 5,
        check_vma=False,
    )
```

profile of v0, /device:TPU:97, one launch (start us, length us, event | category | flops | bytes accessed | tf_op | source)
XLA Modules:
  0.0 171.4 jit_solution(11597373519991181235)
XLA Ops:
  7.2 0.0 copy-start
  7.2 3.3 %collective-permute-start.8 = (bf16[64,512]{1,0:T(8,128)(2,1)}, bf16[64,512]{1,0:T(8,128)(2,1)S(1)}, u32[]{:S(2)}, u32[]{:S(2)}) collective-permute-start(bf16[64,512]{1,0:T(8,128)(2,1)} %bitcast.49), channel_id=1, source_target_pairs={{0,64},{64,128},{128,192},{192,256},{256,320},{320,384},{384,448},... | collective-permute-start | bytes 196616 | tf_op jit(solution)/shard_map/ppermute | solution.py:228
  10.4 10.7 %collective-permute-done.8 = bf16[64,512]{1,0:T(8,128)(2,1)S(1)} collective-permute-done((bf16[64,512]{1,0:T(8,128)(2,1)}, bf16[64,512]{1,0:T(8,128)(2,1)S(1)}, u32[]{:S(2)}, u32[]{:S(2)}) %collective-permute-start.8) | collective-permute-done | bytes 65568 | tf_op jit(solution)/shard_map/ppermute | solution.py:228
  21.1 0.7 broadcast_in_dim.22
  21.8 5.9 %all-to-all-start.1 = ((bf16[4,64,512]{2,1,0:T(8,128)(2,1)}), bf16[4,64,512]{2,1,0:T(8,128)(2,1)S(1)}, u32[]{:S(2)}, u32[]{:S(2)}) async-start(bf16[4,64,512]{2,1,0:T(8,128)(2,1)} %broadcast_in_dim.22), calls=%async_computation.1 | async-start | bytes 524288 | tf_op jit(solution)/shard_map/all_to_all | solution.py:233
  27.7 0.0 all-gather.2.cloned.1.call-start
  27.7 0.9 pad_maximum_fusion.1
  28.6 5.3 %all-to-all-done.1 = bf16[4,64,512]{2,1,0:T(8,128)(2,1)S(1)} async-done(((bf16[4,64,512]{2,1,0:T(8,128)(2,1)}), bf16[4,64,512]{2,1,0:T(8,128)(2,1)S(1)}, u32[]{:S(2)}, u32[]{:S(2)}) %all-to-all-start.1) | async-done | bytes 262176 | tf_op jit(solution)/shard_map/all_to_all | solution.py:233
  33.9 12.9 %all_to_all.10 = bf16[4,64,768]{2,1,0:T(8,128)(2,1)S(1)} all-to-all(bf16[4,64,768]{2,1,0:T(8,128)(2,1)S(1)} %broadcast_in_dim.21), channel_id=1, replica_groups=mesh['zh'=2,'x'=4,'y'=8,'zl'=4,'c'=2] {'zl'}, dimensions={0} | all-to-all | bytes 786432 | tf_op jit(solution)/shard_map/all_to_all | solution.py:233
  46.8 0.9 pad_maximum_fusion
  47.7 0.0 all-gather.2.cloned.1.call-update
  47.7 0.0 copy-done
  47.7 0.0 copy-start.8
  47.8 0.1 slice_bitcast_fusion.1
  47.9 1.9 %collective-permute-start.4 = (bf16[64,4096]{1,0:T(8,128)(2,1)S(1)}, bf16[64,4096]{1,0:T(8,128)(2,1)S(1)}, u32[]{:S(2)}, u32[]{:S(2)}) collective-permute-start(bf16[64,4096]{1,0:T(8,128)(2,1)S(1)} %get-tuple-element.20), channel_id=1, source_target_pairs={{0,64},{64,128},{128,192},{192,0},{256,320},{320,384},{384,448},{4... | collective-permute-start | bytes 1572872 | tf_op jit(solution)/shard_map/ppermute | solution.py:241
  49.8 1.9 %collective-permute-start.5 = (bf16[64,4096]{1,0:T(8,128)(2,1)S(1)}, bf16[64,4096]{1,0:T(8,128)(2,1)}, u32[]{:S(2)}, u32[]{:S(2)}) collective-permute-start(bf16[64,4096]{1,0:T(8,128)(2,1)S(1)} %get-tuple-element.19), channel_id=1, source_target_pairs={{0,64},{64,128},{128,192},{192,0},{256,320},{320,384},{384,448},{4... | collective-permute-start | bytes 1572872 | tf_op jit(solution)/shard_map/ppermute | solution.py:243
  51.7 10.0 %collective-permute-done.4.near_a_ref = bf16[64,4096]{1,0:T(8,128)(2,1)S(1)} collective-permute-done((bf16[64,4096]{1,0:T(8,128)(2,1)S(1)}, bf16[64,4096]{1,0:T(8,128)(2,1)S(1)}, u32[]{:S(2)}, u32[]{:S(2)}) %collective-permute-start.4) | collective-permute-done | bytes 524320 | tf_op jit(solution)/shard_map/ppermute | solution.py:241
  61.8 0.0 copy-start.2
  61.8 6.5 %collective-permute-start.6 = (bf16[64,4096]{1,0:T(8,128)(2,1)S(1)}, bf16[64,4096]{1,0:T(8,128)(2,1)S(1)}, u32[]{:S(2)}, u32[]{:S(2)}) collective-permute-start(bf16[64,4096]{1,0:T(8,128)(2,1)S(1)} %collective-permute-done.4.near_a_ref), channel_id=1, source_target_pairs={{0,256},{256,0},{1,257},{257,1},{2,258},{258,2},{3,259},{259,3},{4... | collective-permute-start | bytes 1572872 | tf_op jit(solution)/shard_map/ppermute | solution.py:251
  68.2 0.1 slice_bitcast_fusion
  68.3 1.9 %collective-permute-start.3 = (bf16[128,4096]{1,0:T(8,128)(2,1)S(1)}, bf16[128,4096]{1,0:T(8,128)(2,1)S(1)}, u32[]{:S(2)}, u32[]{:S(2)}) collective-permute-start(bf16[128,4096]{1,0:T(8,128)(2,1)S(1)} %slice_bitcast_fusion), channel_id=1, source_target_pairs={{0,64},{64,128},{128,192},{192,256},{256,320},{320,384},{384,448},... | collective-permute-start | bytes 3145736 | tf_op jit(solution)/shard_map/ppermute | solution.py:242
  70.3 0.0 copy-done.2
  70.3 2.8 %collective-permute-done.5.near_b_ref = bf16[64,4096]{1,0:T(8,128)(2,1)} collective-permute-done((bf16[64,4096]{1,0:T(8,128)(2,1)S(1)}, bf16[64,4096]{1,0:T(8,128)(2,1)}, u32[]{:S(2)}, u32[]{:S(2)}) %collective-permute-start.5) | collective-permute-done | bytes 524320 | tf_op jit(solution)/shard_map/ppermute | solution.py:243
  73.1 2.6 %collective-permute-done.6.far_a_ref = bf16[64,4096]{1,0:T(8,128)(2,1)S(1)} collective-permute-done((bf16[64,4096]{1,0:T(8,128)(2,1)S(1)}, bf16[64,4096]{1,0:T(8,128)(2,1)S(1)}, u32[]{:S(2)}, u32[]{:S(2)}) %collective-permute-start.6) | collective-permute-done | bytes 524320 | tf_op jit(solution)/shard_map/ppermute | solution.py:251
  75.7 0.0 copy-start.3
  75.7 0.8 copy-done.3
  76.5 6.5 %collective-permute-start.7 = (bf16[64,4096]{1,0:T(8,128)(2,1)}, bf16[64,4096]{1,0:T(8,128)(2,1)S(1)}, u32[]{:S(2)}, u32[]{:S(2)}) collective-permute-start(bf16[64,4096]{1,0:T(8,128)(2,1)} %collective-permute-done.5.near_b_ref), channel_id=1, source_target_pairs={{0,256},{256,0},{1,257},{257,1},{2,258},{258,2},{3,259},{259,3},{4... | collective-permute-start | bytes 1572872 | tf_op jit(solution)/shard_map/ppermute | solution.py:253
  83.0 0.0 copy-done.8
  83.0 7.7 %collective-permute-start = (bf16[256,256]{1,0:T(8,128)(2,1)S(1)}, bf16[256,256]{1,0:T(8,128)(2,1)S(1)}, u32[]{:S(2)}, u32[]{:S(2)}) collective-permute-start(bf16[256,256]{1,0:T(8,128)(2,1)S(1)} %bitcast.46), channel_id=1, source_target_pairs={{0,62},{1,63},{2,0},{3,1},{4,2},{5,3},{6,4},{7,5},{8,6},{9,7},{10,... | collective-permute-start | bytes 393224 | tf_op jit(solution)/shard_map/ppermute | solution.py:245
  90.7 13.0 %collective-permute-start.1 = (bf16[256,256]{1,0:T(8,128)(2,1)S(1)}, bf16[256,256]{1,0:T(8,128)(2,1)S(1)}, u32[]{:S(2)}, u32[]{:S(2)}) collective-permute-start(bf16[256,256]{1,0:T(8,128)(2,1)S(1)} %bitcast.47), channel_id=1, source_target_pairs={{0,63},{1,0},{2,1},{3,2},{4,3},{5,4},{6,5},{7,6},{8,7},{9,8},{10,9... | collective-permute-start | bytes 393224 | tf_op jit(solution)/shard_map/ppermute | solution.py:244
  103.7 18.8 %collective-permute-done.far_ref = bf16[256,256]{1,0:T(8,128)(2,1)S(1)} collective-permute-done((bf16[256,256]{1,0:T(8,128)(2,1)S(1)}, bf16[256,256]{1,0:T(8,128)(2,1)S(1)}, u32[]{:S(2)}, u32[]{:S(2)}) %collective-permute-start) | collective-permute-done | bytes 131104 | tf_op jit(solution)/shard_map/ppermute | solution.py:245
  122.5 0.0 copy-start.6
  122.5 1.5 collective-permute-done.1.near_ref
  124.0 0.0 copy-done.6
  124.0 0.7 copy-done.7
  124.6 4.5 %attend.1 = bf16[256,512]{1,0:T(8,128)(2,1)} custom-call(s32[1]{0:T(128)} %bitcast.index_ref, s32[2,64]{1,0:T(2,128)} %bitcast.42, bf16[256,512]{1,0:T(8,128)(2,1)} %bitcast.37, bf16[256,256]{1,0:T(8,128)(2,1)} %copy-done.6, bf16[256,256]{1,0:T(8,128)(2,1)} %copy-done.7, f32[4,256]{1,0:T(4,128)} %bitcast.40, f32[4,256]{1,0:T(4,128)} %bitcast.41, ...), custom_call_target="tpu_custom_call" | custom-call | tf_op jit(solution)/shard_map/attend/pallas_call | solution.py:69
  129.1 1.9 %collective-permute-start.2 = (bf16[256,512]{1,0:T(8,128)(2,1)}, bf16[256,512]{1,0:T(8,128)(2,1)S(1)}, u32[]{:S(2)}, u32[]{:S(2)}) collective-permute-start(bf16[256,512]{1,0:T(8,128)(2,1)} %attend.1), channel_id=1, source_target_pairs={{0,64},{64,128},{128,192},{192,256},{256,320},{320,384},{384,448},... | collective-permute-start | bytes 786440 | tf_op jit(solution)/shard_map/ppermute | solution.py:250
  131.0 0.6 pad_add_fusion.place_ref
  131.6 18.7 %collective-permute-done.2.att_ref = bf16[256,512]{1,0:T(8,128)(2,1)S(1)} collective-permute-done((bf16[256,512]{1,0:T(8,128)(2,1)}, bf16[256,512]{1,0:T(8,128)(2,1)S(1)}, u32[]{:S(2)}, u32[]{:S(2)}) %collective-permute-start.2) | collective-permute-done | bytes 262176 | tf_op jit(solution)/shard_map/ppermute | solution.py:250
  150.3 0.0 copy-start.5
  150.3 0.0 collective-permute-done.3.direct_ref
  150.3 0.0 collective-permute-done.7.far_b_ref
  150.4 0.0 copy-start.4
  150.4 0.0 all-gather.2.cloned.1.call-done.weight_ref
  150.4 0.7 copy-done.5
  151.0 0.4 copy-done.1
  151.4 0.1 copy-done.4
  151.6 12.9 %layer.1 = (bf16[256,512]{1,0:T(8,128)(2,1)}, bf16[256,256]{1,0:T(8,128)(2,1)}, f32[4,256]{1,0:T(4,128)}, f32[4,256]{1,0:T(4,128)}, f32[256,512]{1,0:T(8,128)}) custom-call(s32[2]{0:T(128)} %pad_add_fusion.place_ref, s32[2,64]{1,0:T(2,128)} %bitcast.43, bf16[256,512]{1,0:T(8,128)(2,1)} %copy-done.5, f32[1,4096]{1,0:T(1,128)} %gain_ref.1, ...), custom_call_target="tpu_custom_call" | custom-call | tf_op jit(solution)/shard_map/layer/pallas_call | solution.py:189
  (3 shorter events, 0.0 us)
Async XLA Ops:
  7.2 40.6 %copy-start = (bf16[1,256,4096]{2,1,0:T(8,128)(2,1)S(1)}, bf16[1,256,4096]{2,1,0:T(8,128)(2,1)}, u32[]{:S(2)}) copy-start(bf16[1,256,4096]{2,1,0:T(8,128)(2,1)} %param.11) | copy-start | bytes 6291460
  7.2 13.9 %collective-permute-start.8 = (bf16[64,512]{1,0:T(8,128)(2,1)}, bf16[64,512]{1,0:T(8,128)(2,1)S(1)}, u32[]{:S(2)}, u32[]{:S(2)}) collective-permute-start(bf16[64,512]{1,0:T(8,128)(2,1)} %bitcast.49), channel_id=1, source_target_pairs={{0,64},{64,128},{128,192},{192,256},{256,320},{320,384},{384,448},... | collective-permute-start | bytes 196616 | tf_op jit(solution)/shard_map/ppermute | solution.py:228
  21.8 12.0 %all-to-all-start.1 = ((bf16[4,64,512]{2,1,0:T(8,128)(2,1)}), bf16[4,64,512]{2,1,0:T(8,128)(2,1)S(1)}, u32[]{:S(2)}, u32[]{:S(2)}) async-start(bf16[4,64,512]{2,1,0:T(8,128)(2,1)} %broadcast_in_dim.22), calls=%async_computation.1 | async-start | bytes 524288 | tf_op jit(solution)/shard_map/all_to_all | solution.py:233
  27.7 122.7 %all-gather.2.cloned.1.call-start = ((), (), s32[]{:S(2)}) async-start(), calls=%async_computation.2 | async-start | bytes 11141120 | tf_op jit(solution)/shard_map/all_gather | solution.py:238
  47.7 35.2 %copy-start.8 = (bf16[1,256,256]{2,1,0:T(8,128)(2,1)S(1)}, bf16[1,256,256]{2,1,0:T(8,128)(2,1)}, u32[]{:S(2)}) copy-start(bf16[1,256,256]{2,1,0:T(8,128)(2,1)} %param.13) | copy-start | bytes 393220
  47.9 13.9 %collective-permute-start.4 = (bf16[64,4096]{1,0:T(8,128)(2,1)S(1)}, bf16[64,4096]{1,0:T(8,128)(2,1)S(1)}, u32[]{:S(2)}, u32[]{:S(2)}) collective-permute-start(bf16[64,4096]{1,0:T(8,128)(2,1)S(1)} %get-tuple-element.20), channel_id=1, source_target_pairs={{0,64},{64,128},{128,192},{192,0},{256,320},{320,384},{384,448},{4... | collective-permute-start | bytes 1572872 | tf_op jit(solution)/shard_map/ppermute | solution.py:241
  49.8 23.3 %collective-permute-start.5 = (bf16[64,4096]{1,0:T(8,128)(2,1)S(1)}, bf16[64,4096]{1,0:T(8,128)(2,1)}, u32[]{:S(2)}, u32[]{:S(2)}) collective-permute-start(bf16[64,4096]{1,0:T(8,128)(2,1)S(1)} %get-tuple-element.19), channel_id=1, source_target_pairs={{0,64},{64,128},{128,192},{192,0},{256,320},{320,384},{384,448},{4... | collective-permute-start | bytes 1572872 | tf_op jit(solution)/shard_map/ppermute | solution.py:243
  61.8 8.5 %copy-start.2 = (bf16[64,4096]{1,0:T(8,128)(2,1)}, bf16[64,4096]{1,0:T(8,128)(2,1)S(1)}, u32[]{:S(2)}) copy-start(bf16[64,4096]{1,0:T(8,128)(2,1)S(1)} %collective-permute-done.4.near_a_ref) | copy-start | bytes 1572868
  61.8 13.9 %collective-permute-start.6 = (bf16[64,4096]{1,0:T(8,128)(2,1)S(1)}, bf16[64,4096]{1,0:T(8,128)(2,1)S(1)}, u32[]{:S(2)}, u32[]{:S(2)}) collective-permute-start(bf16[64,4096]{1,0:T(8,128)(2,1)S(1)} %collective-permute-done.4.near_a_ref), channel_id=1, source_target_pairs={{0,256},{256,0},{1,257},{257,1},{2,258},{258,2},{3,259},{259,3},{4... | collective-permute-start | bytes 1572872 | tf_op jit(solution)/shard_map/ppermute | solution.py:251
  68.3 82.0 %collective-permute-start.3 = (bf16[128,4096]{1,0:T(8,128)(2,1)S(1)}, bf16[128,4096]{1,0:T(8,128)(2,1)S(1)}, u32[]{:S(2)}, u32[]{:S(2)}) collective-permute-start(bf16[128,4096]{1,0:T(8,128)(2,1)S(1)} %slice_bitcast_fusion), channel_id=1, source_target_pairs={{0,64},{64,128},{128,192},{192,256},{256,320},{320,384},{384,448},... | collective-permute-start | bytes 3145736 | tf_op jit(solution)/shard_map/ppermute | solution.py:242
  75.7 0.8 copy-start.3
  76.5 73.9 %collective-permute-start.7 = (bf16[64,4096]{1,0:T(8,128)(2,1)}, bf16[64,4096]{1,0:T(8,128)(2,1)S(1)}, u32[]{:S(2)}, u32[]{:S(2)}) collective-permute-start(bf16[64,4096]{1,0:T(8,128)(2,1)} %collective-permute-done.5.near_b_ref), channel_id=1, source_target_pairs={{0,256},{256,0},{1,257},{257,1},{2,258},{258,2},{3,259},{259,3},{4... | collective-permute-start | bytes 1572872 | tf_op jit(solution)/shard_map/ppermute | solution.py:253
  83.0 39.5 %collective-permute-start = (bf16[256,256]{1,0:T(8,128)(2,1)S(1)}, bf16[256,256]{1,0:T(8,128)(2,1)S(1)}, u32[]{:S(2)}, u32[]{:S(2)}) collective-permute-start(bf16[256,256]{1,0:T(8,128)(2,1)S(1)} %bitcast.46), channel_id=1, source_target_pairs={{0,62},{1,63},{2,0},{3,1},{4,2},{5,3},{6,4},{7,5},{8,6},{9,7},{10,... | collective-permute-start | bytes 393224 | tf_op jit(solution)/shard_map/ppermute | solution.py:245
  90.7 33.3 %collective-permute-start.1 = (bf16[256,256]{1,0:T(8,128)(2,1)S(1)}, bf16[256,256]{1,0:T(8,128)(2,1)S(1)}, u32[]{:S(2)}, u32[]{:S(2)}) collective-permute-start(bf16[256,256]{1,0:T(8,128)(2,1)S(1)} %bitcast.47), channel_id=1, source_target_pairs={{0,63},{1,0},{2,1},{3,2},{4,3},{5,4},{6,5},{7,6},{8,7},{9,8},{10,9... | collective-permute-start | bytes 393224 | tf_op jit(solution)/shard_map/ppermute | solution.py:244
  122.5 1.5 copy-start.6
  124.0 0.7 copy-start.7
  129.1 21.2 %collective-permute-start.2 = (bf16[256,512]{1,0:T(8,128)(2,1)}, bf16[256,512]{1,0:T(8,128)(2,1)S(1)}, u32[]{:S(2)}, u32[]{:S(2)}) collective-permute-start(bf16[256,512]{1,0:T(8,128)(2,1)} %attend.1), channel_id=1, source_target_pairs={{0,64},{64,128},{128,192},{192,256},{256,320},{320,384},{384,448},... | collective-permute-start | bytes 786440 | tf_op jit(solution)/shard_map/ppermute | solution.py:250
  150.3 0.7 copy-start.5
  150.3 1.1 copy-start.1
  150.4 1.2 copy-start.4
Sparse Core Ops, SparseCore 0:
  47.9 67.2 all-gather.1
where the time goes:
time: 172 us; the launch traced here: 171 us
  waiting for transfers between devices  70.5 us (41%)
  starting transfers between devices  50.4 us (29%)
  Pallas kernels  17.4 us (10%)
  between operations  14.2 us (8%)
  blocking collectives  12.9 us (8%)
  local copies, waits for them, and re-layouts  3.58 us (2%)
  other arithmetic  2.35 us (1%)
    ppermute x1, waiting for transfers between devices, per_device(): far_block = lax.ppermute(keyvals[0], CTX, ring(count, -2))  18.8 us
    ppermute x1, waiting for transfers between devices, per_device(): attended_sent = lax.ppermute(attended, SECT, ring(NS, 1))  18.7 us
    ppermute x1, starting transfers between devices, per_device(): near_block = lax.ppermute(keyvals[0], CTX, ring(count, -1))  13 us
    all_to_all x1, blocking collectives, along_z(): lax.all_to_all(copies, 'zl', 0, 0, tiled=True).reshape(NZ * SHARD, -1)  12.9 us
    pallas_call x1, Pallas kernels, layer(): pl.pallas_call(layer_kernel, out_shape=(jax.ShapeDtypeStruct((rows, NQ),...  12.9 us
    ppermute x1, waiting for transfers between devices, per_device(): out_shard = lax.ppermute(w_out[0].T, SECT, ring(NS, 1))  10.7 us
    ppermute x1, waiting for transfers between devices, per_device(): near_a = lax.ppermute(resid[0, STARTS[1]:STARTS[2]], SECT, turn)  10 us
    ppermute x1, starting transfers between devices, per_device(): far_block = lax.ppermute(keyvals[0], CTX, ring(count, -2))  7.68 us
  transfers between devices with their start and end apart: 11, of which 8 were waited for; matrix products, arithmetic and copies ran while one was open for 1% of the time, Pallas kernels for 3%

commit v1 on v0

--- a/solution.py
+++ b/solution.py
@@ -14,7 +14,7 @@
 NY, NZ, NC, NS = 8, 4, 2, 8
 SHARD = 64
 NX = 4
-STARTS = (0, 128, 192)
+STARTS = (0, 96, 176)
 BLOCK = NZ * NC * SHARD
 NQ = QHEADS * HEAD
 NKV = 2 * HEAD
@@ -91,10 +91,10 @@
     att_ref,
     gain_ref,
     direct_ref,
-    near_a_ref,
-    near_b_ref,
-    far_a_ref,
-    far_b_ref,
+    near_ref,
+    far_ref,
+    first_ref,
+    second_ref,
     weight_ref,
     query_ref,
     keyval_ref,
@@ -107,7 +107,6 @@
     out_sems,
 ):
     rows = query_ref.shape[0]
-    by_near = place_ref[1] > 0
 
     def out_copy(y):
         block = pl.ds(y * BLOCK, BLOCK)
@@ -120,19 +119,20 @@
     out_copy(0).start()
     row_copy(direct_ref, 0).start()
 
-    @pl.when(by_near)
-    def _():
-        row_copy(near_a_ref, 1).start()
-        row_copy(near_b_ref, 2).start()
-
-    @pl.when(jnp.logical_not(by_near))
-    def _():
-        row_copy(far_a_ref, 1).start()
-        row_copy(far_b_ref, 2).start()
+    for part, one, other in ((1, near_ref, far_ref), (2, first_ref, second_ref)):
+        chosen = place_ref[part] > 0
+
+        @pl.when(chosen)
+        def _():
+            row_copy(one, part).start()
+
+        @pl.when(jnp.logical_not(chosen))
+        def _():
+            row_copy(other, part).start()
 
     for y in range(1, NY):
         out_copy(y).start()
-    for part, source in enumerate((direct_ref, near_a_ref, near_b_ref)):
+    for part, source in enumerate((direct_ref, near_ref, first_ref)):
         row_copy(source, part).wait()
 
     total = None
@@ -238,9 +238,11 @@
     weights = lax.all_gather(shards, ("y", "c"), axis=0, tiled=True)
 
     turn = [(s, (s + 1) % NX + s // NX * NX) for s in range(NS)]
-    near_a = lax.ppermute(resid[0, STARTS[1] : STARTS[2]], SECT, turn)
+    near = lax.ppermute(resid[0, STARTS[1] : STARTS[2]], SECT, turn)
     direct = lax.ppermute(resid[0, : STARTS[1]], SECT, ring(NS, 1))
-    near_b = lax.ppermute(resid[0, STARTS[2] :], SECT, turn)
+    rest = resid[0, STARTS[2] :]
+    back = [(s, s + 1) for s in range(0, NS, 2)] + [(s, s - 1) for s in range(NX - 1, NS, NX)]
+    first = lax.ppermute(rest, SECT, [pair for pair in back if pair[0] % NX != NX - 3])
     near_block = lax.ppermute(keyvals[0], CTX, ring(count, -1))
     far_block = lax.ppermute(keyvals[0], CTX, ring(count, -2))
     attended = attend(
@@ -248,12 +250,13 @@
         run_max[0].T, run_sum[0].T, run_out[0],
     )
     attended_sent = lax.ppermute(attended, SECT, ring(NS, 1))
-    far_a = lax.ppermute(near_a, SECT, [(0, NX), (NX, 0)])
-    leaving_b, far_a = lax.optimization_barrier((near_b, far_a))
-    far_b = lax.ppermute(leaving_b, SECT, [(0, NX), (NX, 0)])
-    place = jnp.stack([my_index, (my_x > 0).astype(jnp.int32)])
+    far = lax.ppermute(near, SECT, [(0, NX), (NX, 0)])
+    on = [(s, s + 1) for s in range(1, NS, NX)] + [(s, (s + 2) % NS) for s in range(2, NS, NX)]
+    passing = jnp.where(my_x == 2, first, rest)
+    second = lax.ppermute(passing, SECT, on)
+    place = jnp.stack([my_index, (my_x > 0).astype(jnp.int32), my_x % 2])
     query_new, keyval_new, max_new, sum_new, out_new = layer(
-        place, spans, attended_sent, norm_gain, (direct, near_a, near_b, far_a, far_b), weights
+        place, spans, attended_sent, norm_gain, (direct, near, far, first, second), weights
     )
     return (query_new[None], keyval_new[None], max_new.T[None], sum_new.T[None], out_new[None])
 

time: 172 us -> 191 us (1.11)
  the two profiles are of different devices: /device:TPU:97 before, /device:TPU:96 now
where the time goes in v1:
time: 191 us
  waiting for transfers between devices  108 us (57%)
  starting transfers between devices  29.2 us (15%)
  Pallas kernels  17.4 us (9%)
  between operations  14.2 us (7%)
  blocking collectives  13.5 us (7%)
  local copies, waits for them, and re-layouts  4.85 us (3%)
  other arithmetic  3.41 us (2%)
    ppermute x1, waiting for transfers between devices, per_device(): near = lax.ppermute(resid[0, STARTS[1]:STARTS[2]], SECT, turn)  36.9 us
    ppermute x1, waiting for transfers between devices, per_device(): attended_sent = lax.ppermute(attended, SECT, ring(NS, 1))  15.7 us
    ppermute x1, waiting for transfers between devices, per_device(): near_block = lax.ppermute(keyvals[0], CTX, ring(count, -1))  14.7 us
    ppermute x1, waiting for transfers between devices, per_device(): far_block = lax.ppermute(keyvals[0], CTX, ring(count, -2))  13.7 us
    all_to_all x1, blocking collectives, along_z(): lax.all_to_all(copies, 'zl', 0, 0, tiled=True).reshape(NZ * SHARD, -1)  13.5 us
    pallas_call x1, Pallas kernels, layer(): pl.pallas_call(layer_kernel, out_shape=(jax.ShapeDtypeStruct((rows, NQ),...  12.9 us
    ppermute x1, waiting for transfers between devices, per_device(): out_shard = lax.ppermute(w_out[0].T, SECT, ring(NS, 1))  11.3 us
    ppermute x1, waiting for transfers between devices, per_device(): lax.ppermute(rest, SECT, [pair for pair in back if pair[0] % NX != NX - 3])  9.57 us
  transfers between devices with their start and end apart: 11, of which 7 were waited for; matrix products, arithmetic and copies ran while one was open for 2% of the time, Pallas kernels for 2%

profile of v1, /device:TPU:96, one launch (start us, length us, event | category | flops | bytes accessed | tf_op | source)
XLA Modules:
  0.0 190.7 jit_solution(8226916610729548094)
XLA Ops:
  7.2 0.0 copy-start
  7.2 3.5 %collective-permute-start.8 = (bf16[64,512]{1,0:T(8,128)(2,1)}, bf16[64,512]{1,0:T(8,128)(2,1)S(1)}, u32[]{:S(2)}, u32[]{:S(2)}) collective-permute-start(bf16[64,512]{1,0:T(8,128)(2,1)} %bitcast.52), channel_id=1, source_target_pairs={{0,64},{64,128},{128,192},{192,256},{256,320},{320,384},{384,448},... | collective-permute-start | bytes 196616 | tf_op jit(solution)/shard_map/ppermute | solution.py:228
  10.7 11.3 %collective-permute-done.8 = bf16[64,512]{1,0:T(8,128)(2,1)S(1)} collective-permute-done((bf16[64,512]{1,0:T(8,128)(2,1)}, bf16[64,512]{1,0:T(8,128)(2,1)S(1)}, u32[]{:S(2)}, u32[]{:S(2)}) %collective-permute-start.8) | collective-permute-done | bytes 65568 | tf_op jit(solution)/shard_map/ppermute | solution.py:228
  22.0 0.7 broadcast_in_dim.22
  22.7 5.5 %all-to-all-start.1 = ((bf16[4,64,512]{2,1,0:T(8,128)(2,1)}), bf16[4,64,512]{2,1,0:T(8,128)(2,1)S(1)}, u32[]{:S(2)}, u32[]{:S(2)}) async-start(bf16[4,64,512]{2,1,0:T(8,128)(2,1)} %broadcast_in_dim.22), calls=%async_computation.1 | async-start | bytes 524288 | tf_op jit(solution)/shard_map/all_to_all | solution.py:233
  28.2 0.0 all-gather.2.cloned.1.call-start
  28.2 0.9 pad_maximum_fusion.1
  29.1 6.2 %all-to-all-done.1 = bf16[4,64,512]{2,1,0:T(8,128)(2,1)S(1)} async-done(((bf16[4,64,512]{2,1,0:T(8,128)(2,1)}), bf16[4,64,512]{2,1,0:T(8,128)(2,1)S(1)}, u32[]{:S(2)}, u32[]{:S(2)}) %all-to-all-start.1) | async-done | bytes 262176 | tf_op jit(solution)/shard_map/all_to_all | solution.py:233
  35.3 13.5 %all_to_all.10 = bf16[4,64,768]{2,1,0:T(8,128)(2,1)S(1)} all-to-all(bf16[4,64,768]{2,1,0:T(8,128)(2,1)S(1)} %broadcast_in_dim.21), channel_id=1, replica_groups=mesh['zh'=2,'x'=4,'y'=8,'zl'=4,'c'=2] {'zl'}, dimensions={0} | all-to-all | bytes 786432 | tf_op jit(solution)/shard_map/all_to_all | solution.py:233
  48.8 0.9 pad_maximum_fusion
  49.7 0.0 all-gather.2.cloned.1.call-update
  49.7 0.0 copy-done
  49.8 1.2 slice_bitcast_fusion.1
  50.9 1.3 collective-permute-start.6
  52.3 1.0 slice_bitcast_fusion
  53.2 1.9 %collective-permute-start.3 = (bf16[96,4096]{1,0:T(8,128)(2,1)}, bf16[96,4096]{1,0:T(8,128)(2,1)S(1)}, u32[]{:S(2)}, u32[]{:S(2)}) collective-permute-start(bf16[96,4096]{1,0:T(8,128)(2,1)} %slice_bitcast_fusion), channel_id=1, source_target_pairs={{0,64},{64,128},{128,192},{192,256},{256,320},{320,384},{384,448},... | collective-permute-start | bytes 2359304 | tf_op jit(solution)/shard_map/ppermute | solution.py:242
  55.2 2.9 %collective-permute-start.4 = (bf16[80,4096]{1,0:T(8,128)(2,1)}, bf16[80,4096]{1,0:T(8,128)(2,1)}, u32[]{:S(2)}, u32[]{:S(2)}) collective-permute-start(bf16[80,4096]{1,0:T(8,128)(2,1)} %get-tuple-element.16), channel_id=1, source_target_pairs={{0,64},{64,128},{128,192},{192,0},{256,320},{320,384},{384,448},{4... | collective-permute-start | bytes 1966088 | tf_op jit(solution)/shard_map/ppermute | solution.py:241
  58.1 9.6 %collective-permute-done.6.first_ref = bf16[80,4096]{1,0:T(8,128)(2,1)S(1)} collective-permute-done((bf16[80,4096]{1,0:T(8,128)(2,1)}, bf16[80,4096]{1,0:T(8,128)(2,1)S(1)}, u32[]{:S(2)}, u32[]{:S(2)}) %collective-permute-start.6) | collective-permute-done | bytes 655392 | tf_op jit(solution)/shard_map/ppermute | solution.py:245
  67.7 0.0 copy-start.1
  67.7 1.0 broadcast_select_fusion
  68.7 1.3 collective-permute-start.7
  69.9 36.9 %collective-permute-done.4.near_ref = bf16[80,4096]{1,0:T(8,128)(2,1)} collective-permute-done((bf16[80,4096]{1,0:T(8,128)(2,1)}, bf16[80,4096]{1,0:T(8,128)(2,1)}, u32[]{:S(2)}, u32[]{:S(2)}) %collective-permute-start.4) | collective-permute-done | bytes 655392 | tf_op jit(solution)/shard_map/ppermute | solution.py:241
  106.8 4.4 %collective-permute-start.5 = (bf16[80,4096]{1,0:T(8,128)(2,1)}, bf16[80,4096]{1,0:T(8,128)(2,1)S(1)}, u32[]{:S(2)}, u32[]{:S(2)}) collective-permute-start(bf16[80,4096]{1,0:T(8,128)(2,1)} %collective-permute-done.4.near_ref), channel_id=1, source_target_pairs={{0,256},{256,0},{1,257},{257,1},{2,258},{258,2},{3,259},{259,3},{4... | collective-permute-start | bytes 1966088 | tf_op jit(solution)/shard_map/ppermute | solution.py:253
  111.2 1.9 %collective-permute-start.1 = (bf16[256,256]{1,0:T(8,128)(2,1)}, bf16[256,256]{1,0:T(8,128)(2,1)S(1)}, u32[]{:S(2)}, u32[]{:S(2)}) collective-permute-start(bf16[256,256]{1,0:T(8,128)(2,1)} %bitcast.49), channel_id=1, source_target_pairs={{0,63},{1,0},{2,1},{3,2},{4,3},{5,4},{6,5},{7,6},{8,7},{9,8},{10,9... | collective-permute-start | bytes 393224 | tf_op jit(solution)/shard_map/ppermute | solution.py:246
  113.1 4.5 %collective-permute-start = (bf16[256,256]{1,0:T(8,128)(2,1)}, bf16[256,256]{1,0:T(8,128)(2,1)S(1)}, u32[]{:S(2)}, u32[]{:S(2)}) collective-permute-start(bf16[256,256]{1,0:T(8,128)(2,1)} %bitcast.50), channel_id=1, source_target_pairs={{0,62},{1,63},{2,0},{3,1},{4,2},{5,3},{6,4},{7,5},{8,6},{9,7},{10,... | collective-permute-start | bytes 393224 | tf_op jit(solution)/shard_map/ppermute | solution.py:247
  117.6 14.7 %collective-permute-done.1.near_ref = bf16[256,256]{1,0:T(8,128)(2,1)S(1)} collective-permute-done((bf16[256,256]{1,0:T(8,128)(2,1)}, bf16[256,256]{1,0:T(8,128)(2,1)S(1)}, u32[]{:S(2)}, u32[]{:S(2)}) %collective-permute-start.1) | collective-permute-done | bytes 131104 | tf_op jit(solution)/shard_map/ppermute | solution.py:246
  132.3 0.0 copy-start.6
  132.3 13.7 %collective-permute-done.far_ref = bf16[256,256]{1,0:T(8,128)(2,1)S(1)} collective-permute-done((bf16[256,256]{1,0:T(8,128)(2,1)}, bf16[256,256]{1,0:T(8,128)(2,1)S(1)}, u32[]{:S(2)}, u32[]{:S(2)}) %collective-permute-start) | collective-permute-done | bytes 131104 | tf_op jit(solution)/shard_map/ppermute | solution.py:247
  146.1 0.0 copy-start.7
  146.1 0.0 copy-done.6
  146.1 0.7 copy-done.7
  146.7 4.5 %attend.1 = bf16[256,512]{1,0:T(8,128)(2,1)} custom-call(s32[1]{0:T(128)} %bitcast.index_ref, s32[2,64]{1,0:T(2,128)} %bitcast.45, bf16[256,512]{1,0:T(8,128)(2,1)} %bitcast.40, bf16[256,256]{1,0:T(8,128)(2,1)} %copy-done.7, bf16[256,256]{1,0:T(8,128)(2,1)} %copy-done.6, f32[4,256]{1,0:T(4,128)} %bitcast.43, f32[4,256]{1,0:T(4,128)} %bitcast.44, ...), custom_call_target="tpu_custom_call" | custom-call | tf_op jit(solution)/shard_map/attend/pallas_call | solution.py:69
  151.2 1.9 %collective-permute-start.2 = (bf16[256,512]{1,0:T(8,128)(2,1)}, bf16[256,512]{1,0:T(8,128)(2,1)S(1)}, u32[]{:S(2)}, u32[]{:S(2)}) collective-permute-start(bf16[256,512]{1,0:T(8,128)(2,1)} %attend.1), channel_id=1, source_target_pairs={{0,64},{64,128},{128,192},{192,256},{256,320},{320,384},{384,448},... | collective-permute-start | bytes 786440 | tf_op jit(solution)/shard_map/ppermute | solution.py:252
  153.1 0.7 pad_add_fusion.place_ref
  153.8 15.7 %collective-permute-done.2.att_ref = bf16[256,512]{1,0:T(8,128)(2,1)S(1)} collective-permute-done((bf16[256,512]{1,0:T(8,128)(2,1)}, bf16[256,512]{1,0:T(8,128)(2,1)S(1)}, u32[]{:S(2)}, u32[]{:S(2)}) %collective-permute-start.2) | collective-permute-done | bytes 262176 | tf_op jit(solution)/shard_map/ppermute | solution.py:252
  169.5 0.0 copy-start.5
  169.5 0.0 collective-permute-done.3.direct_ref
  169.5 0.0 collective-permute-done.7.second_ref
  169.5 0.0 copy-start.3
  169.5 0.0 collective-permute-done.5.far_ref
  169.5 0.0 copy-start.4
  169.6 0.0 all-gather.2.cloned.1.call-done.weight_ref
  169.6 0.0 copy-done.1
  169.6 0.6 copy-done.5
  170.2 0.3 copy-done.2
  170.5 0.2 copy-done.3
  170.7 0.2 copy-done.4
  170.9 12.9 %layer.1 = (bf16[256,512]{1,0:T(8,128)(2,1)}, bf16[256,256]{1,0:T(8,128)(2,1)}, f32[4,256]{1,0:T(4,128)}, f32[4,256]{1,0:T(4,128)}, f32[256,512]{1,0:T(8,128)}) custom-call(s32[3]{0:T(128)} %pad_add_fusion.place_ref, s32[2,64]{1,0:T(2,128)} %bitcast.46, bf16[256,512]{1,0:T(8,128)(2,1)} %copy-done.5, f32[1,4096]{1,0:T(1,128)} %gain_ref.1, ...), custom_call_target="tpu_custom_call" | custom-call | tf_op jit(solution)/shard_map/layer/pallas_call | solution.py:189
  (2 shorter events, 0.0 us)
Async XLA Ops:
  7.2 42.6 %copy-start = (bf16[1,256,4096]{2,1,0:T(8,128)(2,1)S(1)}, bf16[1,256,4096]{2,1,0:T(8,128)(2,1)}, u32[]{:S(2)}) copy-start(bf16[1,256,4096]{2,1,0:T(8,128)(2,1)} %param.11) | copy-start | bytes 6291460
  7.2 14.8 %collective-permute-start.8 = (bf16[64,512]{1,0:T(8,128)(2,1)}, bf16[64,512]{1,0:T(8,128)(2,1)S(1)}, u32[]{:S(2)}, u32[]{:S(2)}) collective-permute-start(bf16[64,512]{1,0:T(8,128)(2,1)} %bitcast.52), channel_id=1, source_target_pairs={{0,64},{64,128},{128,192},{192,256},{256,320},{320,384},{384,448},... | collective-permute-start | bytes 196616 | tf_op jit(solution)/shard_map/ppermute | solution.py:228
  22.7 12.6 %all-to-all-start.1 = ((bf16[4,64,512]{2,1,0:T(8,128)(2,1)}), bf16[4,64,512]{2,1,0:T(8,128)(2,1)S(1)}, u32[]{:S(2)}, u32[]{:S(2)}) async-start(bf16[4,64,512]{2,1,0:T(8,128)(2,1)} %broadcast_in_dim.22), calls=%async_computation.1 | async-start | bytes 524288 | tf_op jit(solution)/shard_map/all_to_all | solution.py:233
  28.2 141.4 %all-gather.2.cloned.1.call-start = ((), (), s32[]{:S(2)}) async-start(), calls=%async_computation.2 | async-start | bytes 11141120 | tf_op jit(solution)/shard_map/all_gather | solution.py:238
  50.9 16.7 %collective-permute-start.6 = (bf16[80,4096]{1,0:T(8,128)(2,1)}, bf16[80,4096]{1,0:T(8,128)(2,1)S(1)}, u32[]{:S(2)}, u32[]{:S(2)}) collective-permute-start(bf16[80,4096]{1,0:T(8,128)(2,1)} %get-tuple-element.15), channel_id=1, source_target_pairs={{0,64},{128,192},{256,320},{384,448},{192,128},{448,384},{1,65},{1... | collective-permute-start | bytes 1966088 | tf_op jit(solution)/shard_map/ppermute | solution.py:245
  53.2 116.3 %collective-permute-start.3 = (bf16[96,4096]{1,0:T(8,128)(2,1)}, bf16[96,4096]{1,0:T(8,128)(2,1)S(1)}, u32[]{:S(2)}, u32[]{:S(2)}) collective-permute-start(bf16[96,4096]{1,0:T(8,128)(2,1)} %slice_bitcast_fusion), channel_id=1, source_target_pairs={{0,64},{64,128},{128,192},{192,256},{256,320},{320,384},{384,448},... | collective-permute-start | bytes 2359304 | tf_op jit(solution)/shard_map/ppermute | solution.py:242
  55.2 51.7 %collective-permute-start.4 = (bf16[80,4096]{1,0:T(8,128)(2,1)}, bf16[80,4096]{1,0:T(8,128)(2,1)}, u32[]{:S(2)}, u32[]{:S(2)}) collective-permute-start(bf16[80,4096]{1,0:T(8,128)(2,1)} %get-tuple-element.16), channel_id=1, source_target_pairs={{0,64},{64,128},{128,192},{192,0},{256,320},{320,384},{384,448},{4... | collective-permute-start | bytes 1966088 | tf_op jit(solution)/shard_map/ppermute | solution.py:241
  67.7 101.9 %copy-start.1 = (bf16[80,4096]{1,0:T(8,128)(2,1)}, bf16[80,4096]{1,0:T(8,128)(2,1)S(1)}, u32[]{:S(2)}) copy-start(bf16[80,4096]{1,0:T(8,128)(2,1)S(1)} %collective-permute-done.6.first_ref) | copy-start | bytes 1966084
  68.7 100.9 %collective-permute-start.7 = (bf16[80,4096]{1,0:T(8,128)(2,1)}, bf16[80,4096]{1,0:T(8,128)(2,1)S(1)}, u32[]{:S(2)}, u32[]{:S(2)}) collective-permute-start(bf16[80,4096]{1,0:T(8,128)(2,1)} %broadcast_select_fusion), channel_id=1, source_target_pairs={{64,128},{320,384},{128,256},{384,0},{65,129},{321,385},{129,257},... | collective-permute-start | bytes 1966088 | tf_op jit(solution)/shard_map/ppermute | solution.py:256
  106.8 62.7 %collective-permute-start.5 = (bf16[80,4096]{1,0:T(8,128)(2,1)}, bf16[80,4096]{1,0:T(8,128)(2,1)S(1)}, u32[]{:S(2)}, u32[]{:S(2)}) collective-permute-start(bf16[80,4096]{1,0:T(8,128)(2,1)} %collective-permute-done.4.near_ref), channel_id=1, source_target_pairs={{0,256},{256,0},{1,257},{257,1},{2,258},{258,2},{3,259},{259,3},{4... | collective-permute-start | bytes 1966088 | tf_op jit(solution)/shard_map/ppermute | solution.py:253
  111.2 21.1 %collective-permute-start.1 = (bf16[256,256]{1,0:T(8,128)(2,1)}, bf16[256,256]{1,0:T(8,128)(2,1)S(1)}, u32[]{:S(2)}, u32[]{:S(2)}) collective-permute-start(bf16[256,256]{1,0:T(8,128)(2,1)} %bitcast.49), channel_id=1, source_target_pairs={{0,63},{1,0},{2,1},{3,2},{4,3},{5,4},{6,5},{7,6},{8,7},{9,8},{10,9... | collective-permute-start | bytes 393224 | tf_op jit(solution)/shard_map/ppermute | solution.py:246
  113.1 32.9 %collective-permute-start = (bf16[256,256]{1,0:T(8,128)(2,1)}, bf16[256,256]{1,0:T(8,128)(2,1)S(1)}, u32[]{:S(2)}, u32[]{:S(2)}) collective-permute-start(bf16[256,256]{1,0:T(8,128)(2,1)} %bitcast.50), channel_id=1, source_target_pairs={{0,62},{1,63},{2,0},{3,1},{4,2},{5,3},{6,4},{7,5},{8,6},{9,7},{10,... | collective-permute-start | bytes 393224 | tf_op jit(solution)/shard_map/ppermute | solution.py:247
  132.3 13.7 %copy-start.6 = (bf16[256,256]{1,0:T(8,128)(2,1)}, bf16[256,256]{1,0:T(8,128)(2,1)S(1)}, u32[]{:S(2)}) copy-start(bf16[256,256]{1,0:T(8,128)(2,1)S(1)} %collective-permute-done.1.near_ref) | copy-start | bytes 393220
  146.1 0.7 copy-start.7
  151.2 18.3 %collective-permute-start.2 = (bf16[256,512]{1,0:T(8,128)(2,1)}, bf16[256,512]{1,0:T(8,128)(2,1)S(1)}, u32[]{:S(2)}, u32[]{:S(2)}) collective-permute-start(bf16[256,512]{1,0:T(8,128)(2,1)} %attend.1), channel_id=1, source_target_pairs={{0,64},{64,128},{128,192},{192,256},{256,320},{320,384},{384,448},... | collective-permute-start | bytes 786440 | tf_op jit(solution)/shard_map/ppermute | solution.py:252
  169.5 0.7 copy-start.5
  169.5 1.0 copy-start.2
  169.5 1.2 copy-start.3
  169.5 1.3 copy-start.4
Sparse Core Ops, SparseCore 0:
  49.9 64.8 all-gather.1

commit v2 on v1

--- a/solution.py
+++ b/solution.py
@@ -14,7 +14,7 @@
 NY, NZ, NC, NS = 8, 4, 2, 8
 SHARD = 64
 NX = 4
-STARTS = (0, 96, 176)
+STARTS = (0, 80, 176)
 BLOCK = NZ * NC * SHARD
 NQ = QHEADS * HEAD
 NKV = 2 * HEAD
@@ -76,12 +76,12 @@
     )(my_index, spans, *operands)
 
 
-def in_order(w_ref, y, cols):
+def in_order(w_ref, y):
     parts = []
     for z in range(NZ):
         for c in range(NC):
             start = ((y * NC + c) * NZ + z) * SHARD
-            parts.append(w_ref[start : start + SHARD, cols])
+            parts.append(w_ref[start : start + SHARD, :])
     return jnp.concatenate(parts, axis=0)
 
 
@@ -103,14 +103,22 @@
     wide_ref,
     resid_ref,
     out_ref,
+    next_ref,
     row_sems,
     out_sems,
+    next_sems,
 ):
     rows = query_ref.shape[0]
 
     def out_copy(y):
         block = pl.ds(y * BLOCK, BLOCK)
-        return pltpu.make_async_copy(weight_ref.at[block, :], out_ref.at[block, :], out_sems.at[y])
+        source = weight_ref.at[block, pl.ds(NQ + NKV, NQ)]
+        return pltpu.make_async_copy(source, out_ref.at[block, :], out_sems.at[y])
+
+    def next_copy(y):
+        block = pl.ds(y * BLOCK, BLOCK)
+        source = weight_ref.at[block, pl.ds(0, NQ + NKV)]
+        return pltpu.make_async_copy(source, next_ref.at[block, :], next_sems.at[y])
 
     def row_copy(source, part):
         block = resid_ref.at[pl.ds(STARTS[part], source.shape[0]), :]
@@ -139,9 +147,10 @@
     for y in range(NY):
         cols = slice(y * BLOCK, (y + 1) * BLOCK)
         out_copy(y).wait()
+        next_copy(y).start()
         projected = lax.dot_general(
             att_ref[...],
-            in_order(out_ref, y, slice(NQ + NKV, None)),
+            in_order(out_ref, y),
             (((1,), (1,)), ((), ())),
             preferred_element_type=jnp.float32,
         )
@@ -157,8 +166,9 @@
     for y in range(NY):
         cols = slice(y * BLOCK, (y + 1) * BLOCK)
         value = resid_ref[:, cols].astype(jnp.float32) * scale * gain_ref[:, cols]
+        next_copy(y).wait()
         part = jnp.dot(
-            value.astype(jnp.bfloat16), in_order(out_ref, y, slice(0, NQ + NKV)), preferred_element_type=jnp.float32
+            value.astype(jnp.bfloat16), in_order(next_ref, y), preferred_element_type=jnp.float32
         )
         total = part if total is None else total + part
 
@@ -199,8 +209,10 @@
         out_specs=(vmem,) * 5,
         scratch_shapes=[
             pltpu.VMEM((rows, depth), jnp.bfloat16),
-            pltpu.VMEM(weights.shape, jnp.bfloat16),
+            pltpu.VMEM((depth, NQ), jnp.bfloat16),
+            pltpu.VMEM((depth, NQ + NKV), jnp.bfloat16),
             pltpu.SemaphoreType.DMA((len(STARTS),)),
+            pltpu.SemaphoreType.DMA((NY,)),
             pltpu.SemaphoreType.DMA((NY,)),
         ],
         name="layer",

time: 191 us -> 168 us (0.88)
  the two profiles are of different devices: /device:TPU:96 before, /device:TPU:32 now
where the time goes in v2:
time: 168 us
  waiting for transfers between devices  91.7 us (55%)
  starting transfers between devices  24.7 us (15%)
  Pallas kernels  16.7 us (10%)
  between operations  14.2 us (8%)
  blocking collectives  13.5 us (8%)
  local copies, waits for them, and re-layouts  3.76 us (2%)
  other arithmetic  3.44 us (2%)
    ppermute x1, waiting for transfers between devices, per_device(): near = lax.ppermute(resid[0, STARTS[1]:STARTS[2]], SECT, turn)  26.3 us
    ppermute x1, waiting for transfers between devices, per_device(): far_block = lax.ppermute(keyvals[0], CTX, ring(count, -2))  23.4 us
    ppermute x1, waiting for transfers between devices, per_device(): attended_sent = lax.ppermute(attended, SECT, ring(NS, 1))  17.1 us
    all_to_all x1, blocking collectives, along_z(): lax.all_to_all(copies, 'zl', 0, 0, tiled=True).reshape(NZ * SHARD, -1)  13.5 us
    pallas_call x1, Pallas kernels, layer(): pl.pallas_call(layer_kernel, out_shape=(jax.ShapeDtypeStruct((rows, NQ),...  12.2 us
    ppermute x1, waiting for transfers between devices, per_device(): out_shard = lax.ppermute(w_out[0].T, SECT, ring(NS, 1))  12.2 us
    all_to_all x1, waiting for transfers between devices, along_z(): lax.all_to_all(copies, 'zl', 0, 0, tiled=True).reshape(NZ * SHARD, -1)  8.07 us
    all_to_all x1, starting transfers between devices, along_z(): lax.all_to_all(copies, 'zl', 0, 0, tiled=True).reshape(NZ * SHARD, -1)  4.98 us
  transfers between devices with their start and end apart: 11, of which 6 were waited for; matrix products, arithmetic and copies ran while one was open for 2% of the time, Pallas kernels for 3%

profile of v2, /device:TPU:32, one launch (start us, length us, event | category | flops | bytes accessed | tf_op | source)
XLA Modules:
  0.0 168.0 jit_solution(2569027268611607863)
XLA Ops:
  7.2 0.0 copy-start
  7.2 3.5 %collective-permute-start.8 = (bf16[64,512]{1,0:T(8,128)(2,1)}, bf16[64,512]{1,0:T(8,128)(2,1)S(1)}, u32[]{:S(2)}, u32[]{:S(2)}) collective-permute-start(bf16[64,512]{1,0:T(8,128)(2,1)} %bitcast.52), channel_id=1, source_target_pairs={{0,64},{64,128},{128,192},{192,256},{256,320},{320,384},{384,448},... | collective-permute-start | bytes 196616 | tf_op jit(solution)/shard_map/ppermute | solution.py:240
  10.7 12.2 %collective-permute-done.8 = bf16[64,512]{1,0:T(8,128)(2,1)S(1)} collective-permute-done((bf16[64,512]{1,0:T(8,128)(2,1)}, bf16[64,512]{1,0:T(8,128)(2,1)S(1)}, u32[]{:S(2)}, u32[]{:S(2)}) %collective-permute-start.8) | collective-permute-done | bytes 65568 | tf_op jit(solution)/shard_map/ppermute | solution.py:240
  22.9 0.7 broadcast_in_dim.22
  23.6 5.0 %all-to-all-start.1 = ((bf16[4,64,512]{2,1,0:T(8,128)(2,1)}), bf16[4,64,512]{2,1,0:T(8,128)(2,1)S(1)}, u32[]{:S(2)}, u32[]{:S(2)}) async-start(bf16[4,64,512]{2,1,0:T(8,128)(2,1)} %broadcast_in_dim.22), calls=%async_computation.1 | async-start | bytes 524288 | tf_op jit(solution)/shard_map/all_to_all | solution.py:245
  28.6 0.0 all-gather.2.cloned.1.call-start
  28.6 0.9 pad_maximum_fusion.1
  29.4 8.1 %all-to-all-done.1 = bf16[4,64,512]{2,1,0:T(8,128)(2,1)S(1)} async-done(((bf16[4,64,512]{2,1,0:T(8,128)(2,1)}), bf16[4,64,512]{2,1,0:T(8,128)(2,1)S(1)}, u32[]{:S(2)}, u32[]{:S(2)}) %all-to-all-start.1) | async-done | bytes 262176 | tf_op jit(solution)/shard_map/all_to_all | solution.py:245
  37.5 13.5 %all_to_all.10 = bf16[4,64,768]{2,1,0:T(8,128)(2,1)S(1)} all-to-all(bf16[4,64,768]{2,1,0:T(8,128)(2,1)S(1)} %broadcast_in_dim.21), channel_id=1, replica_groups=mesh['zh'=2,'x'=4,'y'=8,'zl'=4,'c'=2] {'zl'}, dimensions={0} | all-to-all | bytes 786432 | tf_op jit(solution)/shard_map/all_to_all | solution.py:245
  51.0 0.9 pad_maximum_fusion
  51.9 0.0 all-gather.2.cloned.1.call-update
  51.9 0.0 copy-done
  51.9 0.1 slice_bitcast_fusion
  52.0 1.9 %collective-permute-start.4 = (bf16[96,4096]{1,0:T(8,128)(2,1)S(1)}, bf16[96,4096]{1,0:T(8,128)(2,1)}, u32[]{:S(2)}, u32[]{:S(2)}) collective-permute-start(bf16[96,4096]{1,0:T(8,128)(2,1)S(1)} %slice_bitcast_fusion), channel_id=1, source_target_pairs={{0,64},{64,128},{128,192},{192,0},{256,320},{320,384},{384,448},{4... | collective-permute-start | bytes 2359304 | tf_op jit(solution)/shard_map/ppermute | solution.py:253
  53.9 1.1 slice_bitcast_fusion.1
  55.1 1.3 collective-permute-start.6
  56.4 1.9 %collective-permute-start.3 = (bf16[80,4096]{1,0:T(8,128)(2,1)}, bf16[80,4096]{1,0:T(8,128)(2,1)}, u32[]{:S(2)}, u32[]{:S(2)}) collective-permute-start(bf16[80,4096]{1,0:T(8,128)(2,1)} %get-tuple-element.16), channel_id=1, source_target_pairs={{0,64},{64,128},{128,192},{192,256},{256,320},{320,384},{384,448},... | collective-permute-start | bytes 1966088 | tf_op jit(solution)/shard_map/ppermute | solution.py:254
  58.3 26.3 %collective-permute-done.4.near_ref = bf16[96,4096]{1,0:T(8,128)(2,1)} collective-permute-done((bf16[96,4096]{1,0:T(8,128)(2,1)S(1)}, bf16[96,4096]{1,0:T(8,128)(2,1)}, u32[]{:S(2)}, u32[]{:S(2)}) %collective-permute-start.4) | collective-permute-done | bytes 786464 | tf_op jit(solution)/shard_map/ppermute | solution.py:253
  84.6 4.0 %collective-permute-start.5 = (bf16[96,4096]{1,0:T(8,128)(2,1)}, bf16[96,4096]{1,0:T(8,128)(2,1)S(1)}, u32[]{:S(2)}, u32[]{:S(2)}) collective-permute-start(bf16[96,4096]{1,0:T(8,128)(2,1)} %collective-permute-done.4.near_ref), channel_id=1, source_target_pairs={{0,256},{256,0},{1,257},{257,1},{2,258},{258,2},{3,259},{259,3},{4... | collective-permute-start | bytes 2359304 | tf_op jit(solution)/shard_map/ppermute | solution.py:265
  88.6 0.0 collective-permute-done.6.first_ref
  88.6 0.0 copy-start.1
  88.6 1.0 broadcast_select_fusion
  89.6 1.3 collective-permute-start.7
  90.9 1.9 %collective-permute-start.1 = (bf16[256,256]{1,0:T(8,128)(2,1)}, bf16[256,256]{1,0:T(8,128)(2,1)S(1)}, u32[]{:S(2)}, u32[]{:S(2)}) collective-permute-start(bf16[256,256]{1,0:T(8,128)(2,1)} %bitcast.49), channel_id=1, source_target_pairs={{0,63},{1,0},{2,1},{3,2},{4,3},{5,4},{6,5},{7,6},{8,7},{9,8},{10,9... | collective-permute-start | bytes 393224 | tf_op jit(solution)/shard_map/ppermute | solution.py:258
  92.8 1.9 %collective-permute-start = (bf16[256,256]{1,0:T(8,128)(2,1)}, bf16[256,256]{1,0:T(8,128)(2,1)S(1)}, u32[]{:S(2)}, u32[]{:S(2)}) collective-permute-start(bf16[256,256]{1,0:T(8,128)(2,1)} %bitcast.50), channel_id=1, source_target_pairs={{0,62},{1,63},{2,0},{3,1},{4,2},{5,3},{6,4},{7,5},{8,6},{9,7},{10,... | collective-permute-start | bytes 393224 | tf_op jit(solution)/shard_map/ppermute | solution.py:259
  94.8 4.6 %collective-permute-done.1.near_ref = bf16[256,256]{1,0:T(8,128)(2,1)S(1)} collective-permute-done((bf16[256,256]{1,0:T(8,128)(2,1)}, bf16[256,256]{1,0:T(8,128)(2,1)S(1)}, u32[]{:S(2)}, u32[]{:S(2)}) %collective-permute-start.1) | collective-permute-done | bytes 131104 | tf_op jit(solution)/shard_map/ppermute | solution.py:258
  99.4 0.0 copy-start.5
  99.4 23.4 %collective-permute-done.far_ref = bf16[256,256]{1,0:T(8,128)(2,1)S(1)} collective-permute-done((bf16[256,256]{1,0:T(8,128)(2,1)}, bf16[256,256]{1,0:T(8,128)(2,1)S(1)}, u32[]{:S(2)}, u32[]{:S(2)}) %collective-permute-start) | collective-permute-done | bytes 131104 | tf_op jit(solution)/shard_map/ppermute | solution.py:259
  122.9 0.0 copy-start.6
  122.9 0.0 copy-done.5
  122.9 0.7 copy-done.6
  123.5 4.5 %attend.1 = bf16[256,512]{1,0:T(8,128)(2,1)} custom-call(s32[1]{0:T(128)} %bitcast.index_ref, s32[2,64]{1,0:T(2,128)} %bitcast.45, bf16[256,512]{1,0:T(8,128)(2,1)} %bitcast.40, bf16[256,256]{1,0:T(8,128)(2,1)} %copy-done.6, bf16[256,256]{1,0:T(8,128)(2,1)} %copy-done.5, f32[4,256]{1,0:T(4,128)} %bitcast.43, f32[4,256]{1,0:T(4,128)} %bitcast.44, ...), custom_call_target="tpu_custom_call" | custom-call | tf_op jit(solution)/shard_map/attend/pallas_call | solution.py:69
  128.0 1.9 %collective-permute-start.2 = (bf16[256,512]{1,0:T(8,128)(2,1)}, bf16[256,512]{1,0:T(8,128)(2,1)S(1)}, u32[]{:S(2)}, u32[]{:S(2)}) collective-permute-start(bf16[256,512]{1,0:T(8,128)(2,1)} %attend.1), channel_id=1, source_target_pairs={{0,64},{64,128},{128,192},{192,256},{256,320},{320,384},{384,448},... | collective-permute-start | bytes 786440 | tf_op jit(solution)/shard_map/ppermute | solution.py:264
  129.9 0.7 pad_add_fusion.place_ref
  130.6 17.1 %collective-permute-done.2.att_ref = bf16[256,512]{1,0:T(8,128)(2,1)S(1)} collective-permute-done((bf16[256,512]{1,0:T(8,128)(2,1)}, bf16[256,512]{1,0:T(8,128)(2,1)S(1)}, u32[]{:S(2)}, u32[]{:S(2)}) %collective-permute-start.2) | collective-permute-done | bytes 262176 | tf_op jit(solution)/shard_map/ppermute | solution.py:264
  147.7 0.0 copy-start.4
  147.7 0.0 collective-permute-done.3.direct_ref
  147.7 0.0 collective-permute-done.7.second_ref
  147.7 0.0 copy-start.3
  147.7 0.0 collective-permute-done.5.far_ref
  147.7 0.0 copy-start.2
  147.7 0.0 all-gather.2.cloned.1.call-done.weight_ref
  147.7 0.0 copy-done.1
  147.7 0.6 copy-done.4
  148.3 0.3 copy-done.3
  148.6 0.3 copy-done.2
  148.9 12.2 %layer.1 = (bf16[256,512]{1,0:T(8,128)(2,1)}, bf16[256,256]{1,0:T(8,128)(2,1)}, f32[4,256]{1,0:T(4,128)}, f32[4,256]{1,0:T(4,128)}, f32[256,512]{1,0:T(8,128)}) custom-call(s32[3]{0:T(128)} %pad_add_fusion.place_ref, s32[2,64]{1,0:T(2,128)} %bitcast.46, bf16[256,512]{1,0:T(8,128)(2,1)} %copy-done.4, f32[1,4096]{1,0:T(1,128)} %gain_ref.1, ...), custom_call_target="tpu_custom_call" | custom-call | tf_op jit(solution)/shard_map/layer/pallas_call | solution.py:199
  (1 shorter events, 0.0 us)
Async XLA Ops:
  7.2 44.8 %copy-start = (bf16[1,256,4096]{2,1,0:T(8,128)(2,1)S(1)}, bf16[1,256,4096]{2,1,0:T(8,128)(2,1)}, u32[]{:S(2)}) copy-start(bf16[1,256,4096]{2,1,0:T(8,128)(2,1)} %param.11) | copy-start | bytes 6291460
  7.2 15.7 %collective-permute-start.8 = (bf16[64,512]{1,0:T(8,128)(2,1)}, bf16[64,512]{1,0:T(8,128)(2,1)S(1)}, u32[]{:S(2)}, u32[]{:S(2)}) collective-permute-start(bf16[64,512]{1,0:T(8,128)(2,1)} %bitcast.52), channel_id=1, source_target_pairs={{0,64},{64,128},{128,192},{192,256},{256,320},{320,384},{384,448},... | collective-permute-start | bytes 196616 | tf_op jit(solution)/shard_map/ppermute | solution.py:240
  23.6 13.9 %all-to-all-start.1 = ((bf16[4,64,512]{2,1,0:T(8,128)(2,1)}), bf16[4,64,512]{2,1,0:T(8,128)(2,1)S(1)}, u32[]{:S(2)}, u32[]{:S(2)}) async-start(bf16[4,64,512]{2,1,0:T(8,128)(2,1)} %broadcast_in_dim.22), calls=%async_computation.1 | async-start | bytes 524288 | tf_op jit(solution)/shard_map/all_to_all | solution.py:245
  28.6 119.1 %all-gather.2.cloned.1.call-start = ((), (), s32[]{:S(2)}) async-start(), calls=%async_computation.2 | async-start | bytes 11141120 | tf_op jit(solution)/shard_map/all_gather | solution.py:250
  52.0 32.6 %collective-permute-start.4 = (bf16[96,4096]{1,0:T(8,128)(2,1)S(1)}, bf16[96,4096]{1,0:T(8,128)(2,1)}, u32[]{:S(2)}, u32[]{:S(2)}) collective-permute-start(bf16[96,4096]{1,0:T(8,128)(2,1)S(1)} %slice_bitcast_fusion), channel_id=1, source_target_pairs={{0,64},{64,128},{128,192},{192,0},{256,320},{320,384},{384,448},{4... | collective-permute-start | bytes 2359304 | tf_op jit(solution)/shard_map/ppermute | solution.py:253
  55.1 33.6 %collective-permute-start.6 = (bf16[80,4096]{1,0:T(8,128)(2,1)}, bf16[80,4096]{1,0:T(8,128)(2,1)S(1)}, u32[]{:S(2)}, u32[]{:S(2)}) collective-permute-start(bf16[80,4096]{1,0:T(8,128)(2,1)} %get-tuple-element.15), channel_id=1, source_target_pairs={{0,64},{128,192},{256,320},{384,448},{192,128},{448,384},{1,65},{1... | collective-permute-start | bytes 1966088 | tf_op jit(solution)/shard_map/ppermute | solution.py:257
  56.4 91.3 %collective-permute-start.3 = (bf16[80,4096]{1,0:T(8,128)(2,1)}, bf16[80,4096]{1,0:T(8,128)(2,1)}, u32[]{:S(2)}, u32[]{:S(2)}) collective-permute-start(bf16[80,4096]{1,0:T(8,128)(2,1)} %get-tuple-element.16), channel_id=1, source_target_pairs={{0,64},{64,128},{128,192},{192,256},{256,320},{320,384},{384,448},... | collective-permute-start | bytes 1966088 | tf_op jit(solution)/shard_map/ppermute | solution.py:254
  84.6 63.0 %collective-permute-start.5 = (bf16[96,4096]{1,0:T(8,128)(2,1)}, bf16[96,4096]{1,0:T(8,128)(2,1)S(1)}, u32[]{:S(2)}, u32[]{:S(2)}) collective-permute-start(bf16[96,4096]{1,0:T(8,128)(2,1)} %collective-permute-done.4.near_ref), channel_id=1, source_target_pairs={{0,256},{256,0},{1,257},{257,1},{2,258},{258,2},{3,259},{259,3},{4... | collective-permute-start | bytes 2359304 | tf_op jit(solution)/shard_map/ppermute | solution.py:265
  88.6 59.1 %copy-start.1 = (bf16[80,4096]{1,0:T(8,128)(2,1)}, bf16[80,4096]{1,0:T(8,128)(2,1)S(1)}, u32[]{:S(2)}) copy-start(bf16[80,4096]{1,0:T(8,128)(2,1)S(1)} %collective-permute-done.6.first_ref) | copy-start | bytes 1966084
  89.6 58.0 %collective-permute-start.7 = (bf16[80,4096]{1,0:T(8,128)(2,1)}, bf16[80,4096]{1,0:T(8,128)(2,1)S(1)}, u32[]{:S(2)}, u32[]{:S(2)}) collective-permute-start(bf16[80,4096]{1,0:T(8,128)(2,1)} %broadcast_select_fusion), channel_id=1, source_target_pairs={{64,128},{320,384},{128,256},{384,0},{65,129},{321,385},{129,257},... | collective-permute-start | bytes 1966088 | tf_op jit(solution)/shard_map/ppermute | solution.py:268
  90.9 8.5 %collective-permute-start.1 = (bf16[256,256]{1,0:T(8,128)(2,1)}, bf16[256,256]{1,0:T(8,128)(2,1)S(1)}, u32[]{:S(2)}, u32[]{:S(2)}) collective-permute-start(bf16[256,256]{1,0:T(8,128)(2,1)} %bitcast.49), channel_id=1, source_target_pairs={{0,63},{1,0},{2,1},{3,2},{4,3},{5,4},{6,5},{7,6},{8,7},{9,8},{10,9... | collective-permute-start | bytes 393224 | tf_op jit(solution)/shard_map/ppermute | solution.py:258
  92.8 30.0 %collective-permute-start = (bf16[256,256]{1,0:T(8,128)(2,1)}, bf16[256,256]{1,0:T(8,128)(2,1)S(1)}, u32[]{:S(2)}, u32[]{:S(2)}) collective-permute-start(bf16[256,256]{1,0:T(8,128)(2,1)} %bitcast.50), channel_id=1, source_target_pairs={{0,62},{1,63},{2,0},{3,1},{4,2},{5,3},{6,4},{7,5},{8,6},{9,7},{10,... | collective-permute-start | bytes 393224 | tf_op jit(solution)/shard_map/ppermute | solution.py:259
  99.4 23.4 %copy-start.5 = (bf16[256,256]{1,0:T(8,128)(2,1)}, bf16[256,256]{1,0:T(8,128)(2,1)S(1)}, u32[]{:S(2)}) copy-start(bf16[256,256]{1,0:T(8,128)(2,1)S(1)} %collective-permute-done.1.near_ref) | copy-start | bytes 393220
  122.9 0.7 copy-start.6
  128.0 19.7 %collective-permute-start.2 = (bf16[256,512]{1,0:T(8,128)(2,1)}, bf16[256,512]{1,0:T(8,128)(2,1)S(1)}, u32[]{:S(2)}, u32[]{:S(2)}) collective-permute-start(bf16[256,512]{1,0:T(8,128)(2,1)} %attend.1), channel_id=1, source_target_pairs={{0,64},{64,128},{128,192},{192,256},{256,320},{320,384},{384,448},... | collective-permute-start | bytes 786440 | tf_op jit(solution)/shard_map/ppermute | solution.py:264
  147.7 0.7 copy-start.4
  147.7 0.9 copy-start.3
  147.7 1.2 copy-start.2
Sparse Core Ops, SparseCore 0:
  52.1 67.5 all-gather.1

commit v3 on v2

--- a/solution.py
+++ b/solution.py
@@ -14,7 +14,7 @@
 NY, NZ, NC, NS = 8, 4, 2, 8
 SHARD = 64
 NX = 4
-STARTS = (0, 80, 176)
+STARTS = (0, 96, 176)
 BLOCK = NZ * NC * SHARD
 NQ = QHEADS * HEAD
 NKV = 2 * HEAD
@@ -76,12 +76,14 @@
     )(my_index, spans, *operands)
 
 
-def in_order(w_ref, y):
+def in_order(w_ref, y, slots):
     parts = []
     for z in range(NZ):
         for c in range(NC):
-            start = ((y * NC + c) * NZ + z) * SHARD
-            parts.append(w_ref[start : start + SHARD, :])
+            start = ((y * NC + c) * NZ + slots[z]) * SHARD
+            if not isinstance(start, int):
+                start = pl.multiple_of(start, SHARD)
+            parts.append(w_ref[pl.ds(start, SHARD), :])
     return jnp.concatenate(parts, axis=0)
 
 
@@ -109,6 +111,7 @@
     next_sems,
 ):
     rows = query_ref.shape[0]
+    slots = [lax.rem(place_ref[3] - z + NZ, NZ) for z in range(NZ)]
 
     def out_copy(y):
         block = pl.ds(y * BLOCK, BLOCK)
@@ -150,7 +153,7 @@
         next_copy(y).start()
         projected = lax.dot_general(
             att_ref[...],
-            in_order(out_ref, y),
+            in_order(out_ref, y, slots),
             (((1,), (1,)), ((), ())),
             preferred_element_type=jnp.float32,
         )
@@ -168,7 +171,7 @@
         value = resid_ref[:, cols].astype(jnp.float32) * scale * gain_ref[:, cols]
         next_copy(y).wait()
         part = jnp.dot(
-            value.astype(jnp.bfloat16), in_order(next_ref, y), preferred_element_type=jnp.float32
+            value.astype(jnp.bfloat16), in_order(next_ref, y, range(NZ)), preferred_element_type=jnp.float32
         )
         total = part if total is None else total + part
 
@@ -235,18 +238,19 @@
     count = NY * NZ * NC
     my_index = lax.axis_index(CTX).astype(jnp.int32)
     my_x = lax.axis_index("x").astype(jnp.int32)
+    my_z = lax.axis_index("zl").astype(jnp.int32)
     spans = span_pair.T
 
-    out_shard = lax.ppermute(w_out[0].T, SECT, ring(NS, 1))
+    out_parts = []
+    for k in range(NZ):
+        pairs = [
+            (s * NZ + z, (s + 1) % NS * NZ + (z + k) % NZ) for s in range(NS) for z in range(NZ)
+        ]
+        out_parts.append(lax.ppermute(w_out[0].T, (*SECT, "zl"), pairs))
     next_shard = jnp.concatenate([w_query[0], w_keyval[0]], axis=1)
-
-    def along_z(shard):
-        copies = jnp.broadcast_to(shard, (NZ, *shard.shape))
-        return lax.all_to_all(copies, "zl", 0, 0, tiled=True).reshape(NZ * SHARD, -1)
-
-    next_rows = along_z(next_shard)
-    out_rows = along_z(out_shard)
-    shards = jnp.concatenate([next_rows, out_rows], axis=1)
+    next_copies = jnp.broadcast_to(next_shard, (NZ, SHARD, NQ + NKV))
+    next_rows = lax.all_to_all(next_copies, "zl", 0, 0, tiled=True).reshape(NZ * SHARD, -1)
+    shards = jnp.concatenate([next_rows, jnp.concatenate(out_parts)], axis=1)
     weights = lax.all_gather(shards, ("y", "c"), axis=0, tiled=True)
 
     turn = [(s, (s + 1) % NX + s // NX * NX) for s in range(NS)]
@@ -266,7 +270,7 @@
     on = [(s, s + 1) for s in range(1, NS, NX)] + [(s, (s + 2) % NS) for s in range(2, NS, NX)]
     passing = jnp.where(my_x == 2, first, rest)
     second = lax.ppermute(passing, SECT, on)
-    place = jnp.stack([my_index, (my_x > 0).astype(jnp.int32), my_x % 2])
+    place = jnp.stack([my_index, (my_x > 0).astype(jnp.int32), my_x % 2, my_z])
     query_new, keyval_new, max_new, sum_new, out_new = layer(
         place, spans, attended_sent, norm_gain, (direct, near, far, first, second), weights
     )

time: 168 us -> 174 us (1.036)
  the two profiles are of different devices: /device:TPU:32 before, /device:TPU:1 now
where the time goes in v3:
time: 174 us; the launch traced here: 172 us
  waiting for transfers between devices  78.3 us (45%)
  starting transfers between devices  54.3 us (31%)
  Pallas kernels  16.7 us (10%)
  between operations  14.2 us (8%)
  local copies, waits for them, and re-layouts  4.96 us (3%)
  other arithmetic  3.4 us (2%)
    ppermute x1, waiting for transfers between devices, per_device(): near = lax.ppermute(resid[0, STARTS[1]:STARTS[2]], SECT, turn)  41.9 us
    ppermute x4, starting transfers between devices, per_device(): out_parts.append(lax.ppermute(w_out[0].T, (*SECT, 'zl'), pairs))  19 us
    ppermute x1, waiting for transfers between devices, per_device(): near_block = lax.ppermute(keyvals[0], CTX, ring(count, -1))  14.9 us
    ppermute x1, waiting for transfers between devices, per_device(): attended_sent = lax.ppermute(attended, SECT, ring(NS, 1))  13.5 us
    pallas_call x1, Pallas kernels, layer(): pl.pallas_call(layer_kernel, out_shape=(jax.ShapeDtypeStruct((rows, NQ),...  12.2 us
    all_to_all x1, starting transfers between devices, per_device(): lax.all_to_all(next_copies, 'zl', 0, 0, tiled=True).reshape(NZ * SHARD, -1)  7.93 us
    ppermute x1, starting transfers between devices, per_device(): far_block = lax.ppermute(keyvals[0], CTX, ring(count, -2))  7.84 us
    ppermute x1, starting transfers between devices, per_device(): near_block = lax.ppermute(keyvals[0], CTX, ring(count, -1))  5.56 us
  transfers between devices with their start and end apart: 14, of which 6 were waited for; matrix products, arithmetic and copies ran while one was open for 2% of the time, Pallas kernels for 3%

profile of v3, /device:TPU:1, one launch (start us, length us, event | category | flops | bytes accessed | tf_op | source)
XLA Modules:
  0.0 171.9 jit_solution(15752168016204586161)
XLA Ops:
  7.2 0.0 copy-start.8
  7.2 0.9 pad_maximum_fusion
  8.1 0.8 broadcast_in_dim.18
  8.8 7.9 %all-to-all-start = ((bf16[4,64,768]{2,1,0:T(8,128)(2,1)}), bf16[4,64,768]{2,1,0:T(8,128)(2,1)S(1)}, u32[]{:S(2)}, u32[]{:S(2)}) async-start(bf16[4,64,768]{2,1,0:T(8,128)(2,1)} %broadcast_in_dim.18), calls=%async_computation | async-start | bytes 786432 | tf_op jit(solution)/shard_map/all_to_all | solution.py:252
  16.8 0.0 all-gather.2.cloned.1.call-start
  16.8 0.0 copy-done.8
  16.8 6.1 %collective-permute-start.11 = (bf16[64,512]{1,0:T(8,128)(2,1)S(1)}, bf16[64,512]{1,0:T(8,128)(2,1)S(1)}, u32[]{:S(2)}, u32[]{:S(2)}) collective-permute-start(bf16[64,512]{1,0:T(8,128)(2,1)S(1)} %bitcast.49), channel_id=1, source_target_pairs={{0,70},{2,64},{4,66},{6,68},{64,134},{66,128},{68,130},{70,132},{1... | collective-permute-start | bytes 196616 | tf_op jit(solution)/shard_map/ppermute | solution.py:249
  22.9 2.2 %collective-permute-start.10 = (bf16[64,512]{1,0:T(8,128)(2,1)S(1)}, bf16[64,512]{1,0:T(8,128)(2,1)S(1)}, u32[]{:S(2)}, u32[]{:S(2)}) collective-permute-start(bf16[64,512]{1,0:T(8,128)(2,1)S(1)} %bitcast.50), channel_id=1, source_target_pairs={{0,68},{2,70},{4,64},{6,66},{64,132},{66,134},{68,128},{70,130},{1... | collective-permute-start | bytes 196616 | tf_op jit(solution)/shard_map/ppermute | solution.py:249
  25.1 3.7 %collective-permute-start.9 = (bf16[64,512]{1,0:T(8,128)(2,1)S(1)}, bf16[64,512]{1,0:T(8,128)(2,1)S(1)}, u32[]{:S(2)}, u32[]{:S(2)}) collective-permute-start(bf16[64,512]{1,0:T(8,128)(2,1)S(1)} %bitcast.51), channel_id=1, source_target_pairs={{0,66},{2,68},{4,70},{6,64},{64,130},{66,132},{68,134},{70,128},{1... | collective-permute-start | bytes 196616 | tf_op jit(solution)/shard_map/ppermute | solution.py:249
  28.8 7.0 %collective-permute-start.8 = (bf16[64,512]{1,0:T(8,128)(2,1)S(1)}, bf16[64,512]{1,0:T(8,128)(2,1)S(1)}, u32[]{:S(2)}, u32[]{:S(2)}) collective-permute-start(bf16[64,512]{1,0:T(8,128)(2,1)S(1)} %bitcast.52), channel_id=1, source_target_pairs={{0,64},{2,66},{4,68},{6,70},{64,128},{66,130},{68,132},{70,134},{1... | collective-permute-start | bytes 196616 | tf_op jit(solution)/shard_map/ppermute | solution.py:249
  35.8 0.6 collective-permute-done.11
  36.4 0.0 collective-permute-done.10
  36.4 0.0 collective-permute-done.9
  36.4 3.4 %collective-permute-done.8 = bf16[64,512]{1,0:T(8,128)(2,1)S(1)} collective-permute-done((bf16[64,512]{1,0:T(8,128)(2,1)S(1)}, bf16[64,512]{1,0:T(8,128)(2,1)S(1)}, u32[]{:S(2)}, u32[]{:S(2)}) %collective-permute-start.8) | collective-permute-done | bytes 65568 | tf_op jit(solution)/shard_map/ppermute | solution.py:249
  39.9 0.0 all-to-all-done
  39.9 0.9 maximum_maximum_fusion
  40.7 0.0 all-gather.2.cloned.1.call-update
  40.8 1.2 slice_bitcast_fusion.1
  42.0 1.3 collective-permute-start.6
  43.3 0.9 slice_bitcast_fusion
  44.3 1.9 %collective-permute-start.3 = (bf16[96,4096]{1,0:T(8,128)(2,1)}, bf16[96,4096]{1,0:T(8,128)(2,1)S(1)}, u32[]{:S(2)}, u32[]{:S(2)}) collective-permute-start(bf16[96,4096]{1,0:T(8,128)(2,1)} %slice_bitcast_fusion), channel_id=1, source_target_pairs={{0,64},{64,128},{128,192},{192,256},{256,320},{320,384},{384,448},... | collective-permute-start | bytes 2359304 | tf_op jit(solution)/shard_map/ppermute | solution.py:258
  46.2 4.6 %collective-permute-start.4 = (bf16[80,4096]{1,0:T(8,128)(2,1)}, bf16[80,4096]{1,0:T(8,128)(2,1)}, u32[]{:S(2)}, u32[]{:S(2)}) collective-permute-start(bf16[80,4096]{1,0:T(8,128)(2,1)} %get-tuple-element.16), channel_id=1, source_target_pairs={{0,64},{64,128},{128,192},{192,0},{256,320},{320,384},{384,448},{4... | collective-permute-start | bytes 1966088 | tf_op jit(solution)/shard_map/ppermute | solution.py:257
  50.8 3.9 %collective-permute-done.6.first_ref = bf16[80,4096]{1,0:T(8,128)(2,1)S(1)} collective-permute-done((bf16[80,4096]{1,0:T(8,128)(2,1)}, bf16[80,4096]{1,0:T(8,128)(2,1)S(1)}, u32[]{:S(2)}, u32[]{:S(2)}) %collective-permute-start.6) | collective-permute-done | bytes 655392 | tf_op jit(solution)/shard_map/ppermute | solution.py:261
  54.7 1.0 broadcast_select_fusion
  55.7 1.3 collective-permute-start.7
  57.0 41.9 %collective-permute-done.4.near_ref = bf16[80,4096]{1,0:T(8,128)(2,1)} collective-permute-done((bf16[80,4096]{1,0:T(8,128)(2,1)}, bf16[80,4096]{1,0:T(8,128)(2,1)}, u32[]{:S(2)}, u32[]{:S(2)}) %collective-permute-start.4) | collective-permute-done | bytes 655392 | tf_op jit(solution)/shard_map/ppermute | solution.py:257
  98.9 3.0 %collective-permute-start.5 = (bf16[80,4096]{1,0:T(8,128)(2,1)}, bf16[80,4096]{1,0:T(8,128)(2,1)S(1)}, u32[]{:S(2)}, u32[]{:S(2)}) collective-permute-start(bf16[80,4096]{1,0:T(8,128)(2,1)} %collective-permute-done.4.near_ref), channel_id=1, source_target_pairs={{0,256},{256,0},{1,257},{257,1},{2,258},{258,2},{3,259},{259,3},{4... | collective-permute-start | bytes 1966088 | tf_op jit(solution)/shard_map/ppermute | solution.py:269
  101.8 5.6 %collective-permute-start.1 = (bf16[256,256]{1,0:T(8,128)(2,1)}, bf16[256,256]{1,0:T(8,128)(2,1)S(1)}, u32[]{:S(2)}, u32[]{:S(2)}) collective-permute-start(bf16[256,256]{1,0:T(8,128)(2,1)} %bitcast.6), channel_id=1, source_target_pairs={{0,63},{1,0},{2,1},{3,2},{4,3},{5,4},{6,5},{7,6},{8,7},{9,8},{10,9... | collective-permute-start | bytes 393224 | tf_op jit(solution)/shard_map/ppermute | solution.py:262
  107.4 7.8 %collective-permute-start = (bf16[256,256]{1,0:T(8,128)(2,1)}, bf16[256,256]{1,0:T(8,128)(2,1)S(1)}, u32[]{:S(2)}, u32[]{:S(2)}) collective-permute-start(bf16[256,256]{1,0:T(8,128)(2,1)} %bitcast.6), channel_id=1, source_target_pairs={{0,62},{1,63},{2,0},{3,1},{4,2},{5,3},{6,4},{7,5},{8,6},{9,7},{10,... | collective-permute-start | bytes 393224 | tf_op jit(solution)/shard_map/ppermute | solution.py:263
  115.3 14.9 %collective-permute-done.1.near_ref = bf16[256,256]{1,0:T(8,128)(2,1)S(1)} collective-permute-done((bf16[256,256]{1,0:T(8,128)(2,1)}, bf16[256,256]{1,0:T(8,128)(2,1)S(1)}, u32[]{:S(2)}, u32[]{:S(2)}) %collective-permute-start.1) | collective-permute-done | bytes 131104 | tf_op jit(solution)/shard_map/ppermute | solution.py:262
  130.2 0.0 collective-permute-done.far_ref
  130.2 0.6 copy-done.6
  130.8 0.0 copy-done.7
  130.8 4.5 %attend.1 = bf16[256,512]{1,0:T(8,128)(2,1)} custom-call(s32[1]{0:T(128)} %bitcast.index_ref, s32[2,64]{1,0:T(2,128)} %bitcast.44, bf16[256,512]{1,0:T(8,128)(2,1)} %bitcast.39, bf16[256,256]{1,0:T(8,128)(2,1)} %copy-done.7, bf16[256,256]{1,0:T(8,128)(2,1)} %copy-done.6, f32[4,256]{1,0:T(4,128)} %bitcast.42, f32[4,256]{1,0:T(4,128)} %bitcast.43, ...), custom_call_target="tpu_custom_call" | custom-call | tf_op jit(solution)/shard_map/attend/pallas_call | solution.py:69
  135.3 0.0 copy-done.1
  135.3 1.9 %collective-permute-start.2 = (bf16[256,512]{1,0:T(8,128)(2,1)}, bf16[256,512]{1,0:T(8,128)(2,1)S(1)}, u32[]{:S(2)}, u32[]{:S(2)}) collective-permute-start(bf16[256,512]{1,0:T(8,128)(2,1)} %attend.1), channel_id=1, source_target_pairs={{0,64},{64,128},{128,192},{192,256},{256,320},{320,384},{384,448},... | collective-permute-start | bytes 786440 | tf_op jit(solution)/shard_map/ppermute | solution.py:268
  137.2 0.6 pad_add_fusion.place_ref
  137.9 13.5 %collective-permute-done.2.att_ref = bf16[256,512]{1,0:T(8,128)(2,1)S(1)} collective-permute-done((bf16[256,512]{1,0:T(8,128)(2,1)}, bf16[256,512]{1,0:T(8,128)(2,1)S(1)}, u32[]{:S(2)}, u32[]{:S(2)}) %collective-permute-start.2) | collective-permute-done | bytes 262176 | tf_op jit(solution)/shard_map/ppermute | solution.py:268
  151.4 0.0 collective-permute-done.3.direct_ref
  151.4 0.0 collective-permute-done.7.second_ref
  151.5 0.0 collective-permute-done.5.far_ref
  151.5 0.0 copy-start.4
  151.5 0.0 all-gather.2.cloned.1.call-done.weight_ref
  151.5 0.6 copy-done.5
  152.1 0.3 copy-done.2
  152.4 0.2 copy-done.3
  152.6 0.2 copy-done.4
  152.8 12.2 %layer.1 = (bf16[256,512]{1,0:T(8,128)(2,1)}, bf16[256,256]{1,0:T(8,128)(2,1)}, f32[4,256]{1,0:T(4,128)}, f32[4,256]{1,0:T(4,128)}, f32[256,512]{1,0:T(8,128)}) custom-call(s32[4]{0:T(128)} %pad_add_fusion.place_ref, s32[2,64]{1,0:T(2,128)} %bitcast.45, bf16[256,512]{1,0:T(8,128)(2,1)} %copy-done.5, f32[1,4096]{1,0:T(1,128)} %gain_ref.1, ...), custom_call_target="tpu_custom_call" | custom-call | tf_op jit(solution)/shard_map/layer/pallas_call | solution.py:202
  (8 shorter events, 0.0 us)
Async XLA Ops:
  7.2 9.6 %copy-start.8 = (bf16[1,512,64]{1,2,0:T(8,128)(2,1)S(1)}, bf16[1,512,64]{1,2,0:T(8,128)(2,1)}, u32[]{:S(2)}) copy-start(bf16[1,512,64]{1,2,0:T(8,128)(2,1)} %param.21) | copy-start | bytes 196612
  8.8 31.9 %copy-start = (bf16[1,256,4096]{2,1,0:T(8,128)(2,1)S(1)}, bf16[1,256,4096]{2,1,0:T(8,128)(2,1)}, u32[]{:S(2)}) copy-start(bf16[1,256,4096]{2,1,0:T(8,128)(2,1)} %param.11) | copy-start | bytes 6291460
  8.8 31.0 %all-to-all-start = ((bf16[4,64,768]{2,1,0:T(8,128)(2,1)}), bf16[4,64,768]{2,1,0:T(8,128)(2,1)S(1)}, u32[]{:S(2)}, u32[]{:S(2)}) async-start(bf16[4,64,768]{2,1,0:T(8,128)(2,1)} %broadcast_in_dim.18), calls=%async_computation | async-start | bytes 786432 | tf_op jit(solution)/shard_map/all_to_all | solution.py:252
  16.8 134.7 %all-gather.2.cloned.1.call-start = ((), (), s32[]{:S(2)}) async-start(), calls=%async_computation.1 | async-start | bytes 11141120 | tf_op jit(solution)/shard_map/all_gather | solution.py:254
  16.8 19.6 %collective-permute-start.11 = (bf16[64,512]{1,0:T(8,128)(2,1)S(1)}, bf16[64,512]{1,0:T(8,128)(2,1)S(1)}, u32[]{:S(2)}, u32[]{:S(2)}) collective-permute-start(bf16[64,512]{1,0:T(8,128)(2,1)S(1)} %bitcast.49), channel_id=1, source_target_pairs={{0,70},{2,64},{4,66},{6,68},{64,134},{66,128},{68,130},{70,132},{1... | collective-permute-start | bytes 196616 | tf_op jit(solution)/shard_map/ppermute | solution.py:249
  22.9 13.5 %collective-permute-start.10 = (bf16[64,512]{1,0:T(8,128)(2,1)S(1)}, bf16[64,512]{1,0:T(8,128)(2,1)S(1)}, u32[]{:S(2)}, u32[]{:S(2)}) collective-permute-start(bf16[64,512]{1,0:T(8,128)(2,1)S(1)} %bitcast.50), channel_id=1, source_target_pairs={{0,68},{2,70},{4,64},{6,66},{64,132},{66,134},{68,128},{70,130},{1... | collective-permute-start | bytes 196616 | tf_op jit(solution)/shard_map/ppermute | solution.py:249
  25.1 11.3 %collective-permute-start.9 = (bf16[64,512]{1,0:T(8,128)(2,1)S(1)}, bf16[64,512]{1,0:T(8,128)(2,1)S(1)}, u32[]{:S(2)}, u32[]{:S(2)}) collective-permute-start(bf16[64,512]{1,0:T(8,128)(2,1)S(1)} %bitcast.51), channel_id=1, source_target_pairs={{0,66},{2,68},{4,70},{6,64},{64,130},{66,132},{68,134},{70,128},{1... | collective-permute-start | bytes 196616 | tf_op jit(solution)/shard_map/ppermute | solution.py:249
  28.8 11.0 %collective-permute-start.8 = (bf16[64,512]{1,0:T(8,128)(2,1)S(1)}, bf16[64,512]{1,0:T(8,128)(2,1)S(1)}, u32[]{:S(2)}, u32[]{:S(2)}) collective-permute-start(bf16[64,512]{1,0:T(8,128)(2,1)S(1)} %bitcast.52), channel_id=1, source_target_pairs={{0,64},{2,66},{4,68},{6,70},{64,128},{66,130},{68,132},{70,134},{1... | collective-permute-start | bytes 196616 | tf_op jit(solution)/shard_map/ppermute | solution.py:249
  42.0 12.7 %collective-permute-start.6 = (bf16[80,4096]{1,0:T(8,128)(2,1)}, bf16[80,4096]{1,0:T(8,128)(2,1)S(1)}, u32[]{:S(2)}, u32[]{:S(2)}) collective-permute-start(bf16[80,4096]{1,0:T(8,128)(2,1)} %get-tuple-element.15), channel_id=1, source_target_pairs={{0,64},{128,192},{256,320},{384,448},{192,128},{448,384},{1,65},{1... | collective-permute-start | bytes 1966088 | tf_op jit(solution)/shard_map/ppermute | solution.py:261
  44.3 107.2 %collective-permute-start.3 = (bf16[96,4096]{1,0:T(8,128)(2,1)}, bf16[96,4096]{1,0:T(8,128)(2,1)S(1)}, u32[]{:S(2)}, u32[]{:S(2)}) collective-permute-start(bf16[96,4096]{1,0:T(8,128)(2,1)} %slice_bitcast_fusion), channel_id=1, source_target_pairs={{0,64},{64,128},{128,192},{192,256},{256,320},{320,384},{384,448},... | collective-permute-start | bytes 2359304 | tf_op jit(solution)/shard_map/ppermute | solution.py:258
  46.2 52.7 %collective-permute-start.4 = (bf16[80,4096]{1,0:T(8,128)(2,1)}, bf16[80,4096]{1,0:T(8,128)(2,1)}, u32[]{:S(2)}, u32[]{:S(2)}) collective-permute-start(bf16[80,4096]{1,0:T(8,128)(2,1)} %get-tuple-element.16), channel_id=1, source_target_pairs={{0,64},{64,128},{128,192},{192,0},{256,320},{320,384},{384,448},{4... | collective-permute-start | bytes 1966088 | tf_op jit(solution)/shard_map/ppermute | solution.py:257
  54.7 80.6 %copy-start.1 = (bf16[80,4096]{1,0:T(8,128)(2,1)}, bf16[80,4096]{1,0:T(8,128)(2,1)S(1)}, u32[]{:S(2)}) copy-start(bf16[80,4096]{1,0:T(8,128)(2,1)S(1)} %collective-permute-done.6.first_ref) | copy-start | bytes 1966084
  55.7 95.7 %collective-permute-start.7 = (bf16[80,4096]{1,0:T(8,128)(2,1)}, bf16[80,4096]{1,0:T(8,128)(2,1)S(1)}, u32[]{:S(2)}, u32[]{:S(2)}) collective-permute-start(bf16[80,4096]{1,0:T(8,128)(2,1)} %broadcast_select_fusion), channel_id=1, source_target_pairs={{64,128},{320,384},{128,256},{384,0},{65,129},{321,385},{129,257},... | collective-permute-start | bytes 1966088 | tf_op jit(solution)/shard_map/ppermute | solution.py:272
  98.9 52.6 %collective-permute-start.5 = (bf16[80,4096]{1,0:T(8,128)(2,1)}, bf16[80,4096]{1,0:T(8,128)(2,1)S(1)}, u32[]{:S(2)}, u32[]{:S(2)}) collective-permute-start(bf16[80,4096]{1,0:T(8,128)(2,1)} %collective-permute-done.4.near_ref), channel_id=1, source_target_pairs={{0,256},{256,0},{1,257},{257,1},{2,258},{258,2},{3,259},{259,3},{4... | collective-permute-start | bytes 1966088 | tf_op jit(solution)/shard_map/ppermute | solution.py:269
  101.8 28.3 %collective-permute-start.1 = (bf16[256,256]{1,0:T(8,128)(2,1)}, bf16[256,256]{1,0:T(8,128)(2,1)S(1)}, u32[]{:S(2)}, u32[]{:S(2)}) collective-permute-start(bf16[256,256]{1,0:T(8,128)(2,1)} %bitcast.6), channel_id=1, source_target_pairs={{0,63},{1,0},{2,1},{3,2},{4,3},{5,4},{6,5},{7,6},{8,7},{9,8},{10,9... | collective-permute-start | bytes 393224 | tf_op jit(solution)/shard_map/ppermute | solution.py:262
  107.4 22.7 %collective-permute-start = (bf16[256,256]{1,0:T(8,128)(2,1)}, bf16[256,256]{1,0:T(8,128)(2,1)S(1)}, u32[]{:S(2)}, u32[]{:S(2)}) collective-permute-start(bf16[256,256]{1,0:T(8,128)(2,1)} %bitcast.6), channel_id=1, source_target_pairs={{0,62},{1,63},{2,0},{3,1},{4,2},{5,3},{6,4},{7,5},{8,6},{9,7},{10,... | collective-permute-start | bytes 393224 | tf_op jit(solution)/shard_map/ppermute | solution.py:263
  130.2 0.7 copy-start.6
  130.2 0.7 copy-start.7
  135.3 16.1 %collective-permute-start.2 = (bf16[256,512]{1,0:T(8,128)(2,1)}, bf16[256,512]{1,0:T(8,128)(2,1)S(1)}, u32[]{:S(2)}, u32[]{:S(2)}) collective-permute-start(bf16[256,512]{1,0:T(8,128)(2,1)} %attend.1), channel_id=1, source_target_pairs={{0,64},{64,128},{128,192},{192,256},{256,320},{320,384},{384,448},... | collective-permute-start | bytes 786440 | tf_op jit(solution)/shard_map/ppermute | solution.py:268
  151.4 0.7 copy-start.5
  151.4 1.0 copy-start.2
  151.5 1.2 copy-start.3
  151.5 1.4 copy-start.4
Sparse Core Ops, SparseCore 0:
  40.9 72.0 all-gather.1
